TPU v7x, 256 devices: a whole 4x4x8 slice. The times are simulated.
256 devices in a mesh: ax: 16 (over z, core), rad: 4 (over x), pit: 4 (over y).
Axes of the slice: x: 4, y: 4, z: 8, core: 2. Of those that a mesh axis runs over, the one named last changes fastest.
Arguments:
- state: float32 [256, 49, 16, 1024], P('ax', None, 'rad', 'pit'), may hold values from -6 to 6
- flux_jac: float32 [3, 7, 7], replicated, may hold values from -2 to 2
- line_coef: float32 [16, 1024], P('rad', 'pit'), may hold values from 200 to 3000
- line_mask: int32 [256, 16, 1024], P('ax', 'rad', 'pit'), may hold values 0 or 1
Outputs:
- state_next: float32 [256, 49, 16, 1024], P('ax', None, 'rad', 'pit')
All inputs are finite; a program needn't handle non-finite values. No bound on the sum of `line_mask` on one device may be relied on, other than what follows from the above.
Results may differ from a plain program's by a relative error of at most 0.0003.
Values sent between devices are 32-bit elements; how exact they have to be, the bound alone decides.
A program may use at most 64 MiB of HBM per device.

v0:
```python
import jax
import jax.numpy as jnp
import numpy as np
from jax import lax
from jax.sharding import PartitionSpec as P

HARM = 7
VARS = 7


blade_freq = 0.6
dissipation = 0.2
courant = 1.0
section_weight = 0.5


def extended(shard, sides, width, wrap):
    for axis, dim in sides:
        devices, length = (lax.axis_size(axis), shard.shape[dim])
        up = [(i, (i + 1) % devices) for i in range(devices if wrap else devices - 1)]
        down = [(j, i) for i, j in up]
        last = lax.slice_in_dim(shard, length - width, length, axis=dim)
        leading = lax.slice_in_dim(shard, 0, width, axis=dim)
        before = lax.ppermute(last, axis, up)
        after = lax.ppermute(leading, axis, down)
        shard = jnp.concatenate([before, shard, after], axis=dim)
    return shard


def carried_in(part, axis, combine, identity, reverse):
    count = lax.axis_size(axis)
    place = lax.axis_index(axis)
    ahead = count - 1 - place if reverse else place
    gathered = jax.tree.map(lambda a: lax.all_gather(a, axis), part)
    state = jax.tree.map(lambda a, e: jnp.zeros_like(a) + jnp.asarray(e, a.dtype), part, identity)

    def one(lap, state):
        source = count - 1 - lap if reverse else lap
        return combine(
            state, jax.tree.map(lambda a: lax.dynamic_index_in_dim(a, source, 0, False), gathered)
        )

    return lax.fori_loop(0, ahead, one, state)


def coupling_table():
    coupling = np.zeros((HARM, HARM), np.float32)
    for harmonic in range(1, HARM // 2 + 1):
        coupling[2 * harmonic - 1, 2 * harmonic] = -harmonic * blade_freq
        coupling[2 * harmonic, 2 * harmonic - 1] = harmonic * blade_freq
    return jnp.asarray(coupling)


def flux_of(states, matrix):
    dims_all = states.shape
    by_harmonic = states.reshape(dims_all[0], HARM, VARS, dims_all[2], dims_all[3])
    speeds = 1.0 + 0.5 * jnp.tanh(states[:, 0])
    mixed_flux = jnp.einsum("vw,nhwrp->nhvrp", matrix, by_harmonic, precision=lax.Precision.HIGHEST)
    return mixed_flux.reshape(dims_all) * speeds[:, None]


def residual_of(axial_pad, radial_pad, pitch_pad, center, flux_jac):
    flux_axial = flux_of(axial_pad, flux_jac[0])
    divergence = (flux_axial[2:] - flux_axial[:-2]) * 0.5
    flux_radial = flux_of(radial_pad, flux_jac[1])
    divergence = divergence + (flux_radial[:, :, 2:] - flux_radial[:, :, :-2]) * 0.5
    flux_pitch = flux_of(pitch_pad, flux_jac[2])
    divergence = divergence + (flux_pitch[..., 2:] - flux_pitch[..., :-2]) * 0.5
    neighbours = axial_pad[2:] + axial_pad[:-2] + radial_pad[:, :, 2:] + radial_pad[:, :, :-2]
    neighbours = neighbours + pitch_pad[..., 2:] + pitch_pad[..., :-2]
    dims_all = center.shape
    by_harmonic = center.reshape(dims_all[0], HARM, VARS, dims_all[2], dims_all[3])
    coupled = jnp.einsum(
        "hg,ngvrp->nhvrp", coupling_table(), by_harmonic, precision=lax.Precision.HIGHEST
    )
    return -divergence + dissipation * (neighbours - 6.0 * center) + coupled.reshape(dims_all)


def step_rhs(center, resid, coef, flux_jac):
    limit = jnp.sum(jnp.max(jnp.sum(jnp.abs(flux_jac), axis=2), axis=1))
    speeds = 1.0 + 0.5 * jnp.tanh(center[:, 0])
    radius = speeds * limit + 6.0 * dissipation + HARM // 2 * blade_freq
    factor = section_weight * courant * jnp.sqrt(1.0 + 4.0 * coef) / radius
    return factor[:, None] * resid


def normalize(mats):
    largest = jnp.maximum(
        jnp.maximum(jnp.abs(mats[0]), jnp.abs(mats[1])),
        jnp.maximum(jnp.abs(mats[2]), jnp.abs(mats[3])),
    )
    return tuple((entry / largest for entry in mats))


def chain_matrices(earlier, later):
    first = later[0] * earlier[0] + later[1] * earlier[2]
    second = later[0] * earlier[1] + later[1] * earlier[3]
    third = later[2] * earlier[0] + later[3] * earlier[2]
    fourth = later[2] * earlier[1] + later[3] * earlier[3]
    return normalize((first, second, third, fourth))


def chain_affine(earlier, later):
    return (later[0] * earlier[0], later[0][None] * earlier[1] + later[1])


def on_device(state, flux_jac, line_coef, line_mask):
    cells = state.shape[0]
    padded = extended(state, (("ax", 0), ("rad", 2)), 1, False)
    axial_pad = padded[:, :, 1:-1, :]
    radial_pad = padded[1:-1]
    pitch_pad = extended(state, (("pit", 3),), 1, True)
    resid = residual_of(axial_pad, radial_pad, pitch_pad, state, flux_jac)
    coef = line_coef[None] * (1.0 + line_mask.astype(jnp.float32))
    rhs = step_rhs(state, resid, coef, flux_jac)
    block_index = lax.axis_index("ax")
    total_cells = lax.axis_size("ax") * cells
    position = (block_index * cells + jnp.arange(cells))[:, None, None]
    lower = jnp.where(position > 0, -coef, 0.0)
    upper = jnp.where(position < total_cells - 1, -coef, 0.0)
    diagonal = 1.0 + 2.0 * coef
    ones_line = jnp.ones(coef.shape[1:], jnp.float32)
    zeros_line = jnp.zeros(coef.shape[1:], jnp.float32)
    zeros_field = jnp.zeros(rhs.shape[1:], jnp.float32)
    identity_mats = (ones_line, zeros_line, zeros_line, ones_line)
    identity_maps = (ones_line, zeros_field)

    def pivot_step(mats, item):
        low, upp, dia = item
        first = upp * mats[2]
        second = upp * mats[3]
        third = -low * mats[0] + dia * mats[2]
        fourth = -low * mats[1] + dia * mats[3]
        return (normalize((first, second, third, fourth)), None)

    composite, unused = lax.scan(pivot_step, identity_mats, (lower, upper, diagonal))
    incoming = carried_in(composite, "ax", chain_matrices, identity_mats, False)
    pivot_in = incoming[1] / incoming[3]

    def forward(carry, item):
        pivot, partial_value, gains = carry
        low, upp, dia, right = item
        denom = dia - low * pivot
        pivot_new = upp / denom
        gain = -low / denom
        partial_new = gain[None] * partial_value + right / denom[None]
        gains_new = gains * gain
        return ((pivot_new, partial_new, gains_new), (pivot_new, partial_new, gains_new))

    unused_end, (pivots, partials, gain_runs) = lax.scan(
        forward, (pivot_in, zeros_field, ones_line), (lower, upper, diagonal, rhs)
    )
    block_forward = (gain_runs[-1], partials[-1])
    forward_in = carried_in(block_forward, "ax", chain_affine, identity_maps, False)[1]
    eliminated = partials + gain_runs[:, None] * forward_in[None]

    def backward(carry, item):
        after, spread = carry
        pivot, partial_value = item
        value = partial_value - pivot[None] * after
        spread_new = -pivot * spread
        return ((value, spread_new), (value, spread_new))

    unused_start, (local_values, spreads) = lax.scan(
        backward, (zeros_field, ones_line), (pivots, eliminated), reverse=True
    )
    block_backward = (spreads[0], local_values[0])
    backward_in = carried_in(block_backward, "ax", chain_affine, identity_maps, True)[1]
    smoothed = local_values + spreads[:, None] * backward_in[None]
    return state + smoothed


def solution(mesh):
    placed = (P("ax", None, "rad", "pit"), P(), P("rad", "pit"), P("ax", "rad", "pit"))
    return jax.shard_map(
        on_device,
        mesh=mesh,
        in_specs=placed,
        out_specs=P("ax", None, "rad", "pit"),
        check_vma=False,
    )
```

profile of v0, /device:TPU:1, one launch (start us, length us, event | category | flops | bytes accessed | tf_op | source)
XLA Modules:
  0.0 489.8 jit_solution(12801795809369152871)
XLA Ops:
  8.3 4.9 %collective-permute-start = (f32[1,49,4,256]{3,2,1,0:T(4,128)}, f32[1,49,4,256]{3,2,1,0:T(4,128)S(1)}, u32[]{:S(2)}, u32[]{:S(2)}) collective-permute-start(f32[1,49,4,256]{3,2,1,0:T(4,128)} %get-tuple-element.654), channel_id=1, source_target_pairs={{0,16},{16,32},{32,48},{48,64},{64,80},{80,96},{96,112},{112,128},... | collective-permute-start | bytes 602120 | tf_op jit(solution)/shard_map/ppermute | solution.py:24
  15.2 4.5 fusion.78
  19.7 2.6 copy.75
  31.1 32.0 %while.104 = (s32[]{:T(128)}, f32[4,256]{1,0:T(4,128)S(1)}, f32[4,256]{1,0:T(4,128)}, f32[4,256]{1,0:T(4,128)S(1)}, f32[4,256]{1,0:T(4,128)S(1)}, /*index=5*/f32...) while((s32[]{:T(128)}, f32[4,256]{1,0:T(4,128)S(1)}, ...), condition=%wide.region_1.0_spmd.clone, body=%wide.region_0.0_spmd.clone.sunk | while | flops 33795 | bytes 86136 | solution.py:136
  63.1 22.1 %all-gather.4 = f32[16,4,256]{2,1,0:T(4,128)} all-gather(f32[1,4,256]{2,1,0:T(4,128)S(1)} %bitcast.224), channel_id=2, replica_groups=mesh['ax'=16,'rad'=4,'pit'=4] {'ax'}, dimensions={0}, use_global_device_ids=true | all-gather | bytes 69632 | tf_op jit(solution)/shard_map/all_gather | solution.py:34
  85.2 16.9 %all-gather.5 = f32[16,4,256]{2,1,0:T(4,128)} all-gather(f32[1,4,256]{2,1,0:T(4,128)} %bitcast.227), channel_id=3, replica_groups=mesh['ax'=16,'rad'=4,'pit'=4] {'ax'}, dimensions={0}, use_global_device_ids=true | all-gather | bytes 69632 | tf_op jit(solution)/shard_map/all_gather | solution.py:34
  102.1 16.7 %all-gather.6 = f32[16,4,256]{2,1,0:T(4,128)} all-gather(f32[1,4,256]{2,1,0:T(4,128)S(1)} %bitcast.225), channel_id=4, replica_groups=mesh['ax'=16,'rad'=4,'pit'=4] {'ax'}, dimensions={0}, use_global_device_ids=true | all-gather | bytes 69632 | tf_op jit(solution)/shard_map/all_gather | solution.py:34
  118.7 16.7 %all-gather.7 = f32[16,4,256]{2,1,0:T(4,128)} all-gather(f32[1,4,256]{2,1,0:T(4,128)S(1)} %bitcast.226), channel_id=5, replica_groups=mesh['ax'=16,'rad'=4,'pit'=4] {'ax'}, dimensions={0}, use_global_device_ids=true | all-gather | bytes 69632 | tf_op jit(solution)/shard_map/all_gather | solution.py:34
  137.9 6.0 %fusion.43 = f32[16,7,7,4,256]{4,1,3,2,0:T(8,128)} fusion(f32[7,7,1,1,1]{1,0,4,3,2:T(8,128)} %constant.169, f32[16,7,7,4,256]{4,3,2,1,0:T(4,128)S(1)} %bitcast.214), kind=kOutput, calls=%fused_computation.88 | convolution fusion | flops 67436544 | bytes 6422724 | tf_op jit(solution)/shard_map/hg,ngvrp->nhvrp/dot_general | solution.py:73
  146.3 5.6 %copy.65 = f32[16,7,7,4,256]{4,0,3,2,1:T(8,128)} copy(f32[16,7,7,4,256]{4,1,3,2,0:T(8,128)} %fusion.43) | data formatting | bytes 6422528 | tf_op jit(solution)/shard_map/hg,ngvrp->nhvrp/transpose | solution.py:73
  151.9 3.3 copy.55
  155.2 3.2 copy.57
  158.4 4.6 pad_maximum_fusion.1
  163.0 8.6 %fusion.34 = f32[16,7,7,4,258]{4,2,3,1,0:T(8,128)S(1)} fusion(f32[16,7,7,4,258]{4,0,3,2,1:T(8,128)S(1)} %bitcast.219, f32[3,7,7]{2,1,0:T(8,128)} %param.18), kind=kOutput, calls=%fused_computation.85 | convolution fusion | flops 67963392 | bytes 6476800 | tf_op jit(solution)/shard_map/vw,nhwrp->nhvrp/dot_general | solution.py:58
  171.6 2.7 copy.59
  174.4 4.1 copy_multiply_fusion
  186.7 3.2 collective-permute-start.2
  191.2 4.0 fusion.40
  197.7 11.3 %collective-permute-done.2 = f32[18,49,1,256]{3,2,1,0:T(1,128)S(1)} collective-permute-done((f32[18,49,1,256]{3,2,1,0:T(1,128)S(1)}, f32[18,49,1,256]{3,2,1,0:T(1,128)S(1)}, u32[]{:S(2)}, u32[]{:S(2)}) %collective-permute-start.2) | collective-permute-done | bytes 903200 | tf_op jit(solution)/shard_map/ppermute | solution.py:24
  209.0 4.2 collective-permute-done.3
  213.2 2.8 pad_maximum_fusion
  216.5 6.9 %fusion.37 = f32[16,7,7,6,256]{4,2,3,1,0:T(8,128)S(1)} fusion(f32[16,7,7,6,256]{4,3,2,1,0:T(8,128)S(1)} %bitcast.220, f32[3,7,7]{2,1,0:T(8,128)S(1)} %copy-done.8), kind=kOutput, calls=%fused_computation.86 | convolution fusion | flops 101154816 | bytes 11243520 | tf_op jit(solution)/shard_map/vw,nhwrp->nhvrp/dot_general | solution.py:58
  228.1 15.2 %fusion.25 = f32[16,49,4,256]{3,2,1,0:T(4,128)} fusion(f32[16,49,4,256]{3,2,1,0:T(4,128)S(1)} %copy-done, f32[16,49,4,1]{3,2,1,0:T(4,128)} %copy.63, f32[16,49,4,1]{3,2,1,0:T(4,128)} %copy.62, f32[18,49,4,256]{3,2,1,0:T(4,128)S(1)} %constant_dynamic-update-slice_fusion, f32[18,49,1,256]{3,2,1,0:T(1,128)S(1)} %collective-permute-done.2, ...), kind=kLoop, calls=%fused_computation.65 | loop fusion | flops 19267584 | bytes 34812416 | tf_op jit(solution)/shard_map/mul | solution.py:84
  246.1 59.3 %while.105 = (s32[]{:T(128)}, f32[4,256]{1,0:T(4,128)S(1)}, f32[49,4,256]{2,1,0:T(4,128)S(1)}, f32[4,256]{1,0:T(4,128)S(1)}, f32[16,4,256]{2,1,0:T(4,128)}, /*in...) while((s32[]{:T(128)}, f32[4,256]{1,0:T(4,128)S(1)}, ...), condition=%wide.region_8.9_spmd.clone, body=%wide.region_7.8_spmd.clone.sunk | while | flops 207875 | bytes 861324 | solution.py:150
  307.1 34.1 %all_gather.44 = f32[16,4,256]{2,1,0:T(4,128)S(1)} all-gather(f32[1,4,256]{2,1,0:T(4,128)S(1)} %slice.125), channel_id=1, replica_groups=mesh['ax'=16,'rad'=4,'pit'=4] {'ax'}, dimensions={0}, use_global_device_ids=true | all-gather | bytes 69632 | tf_op jit(solution)/shard_map/all_gather | solution.py:34
  341.2 20.6 %all-gather.11.cloned.1.call-done = f32[16,49,4,256]{3,2,1,0:T(4,128)} async-done(((f32[1,49,4,256]{3,2,1,0:T(4,128)}), f32[16,49,4,256]{3,2,1,0:T(4,128)}) %all-gather.11.cloned.1.call-update) | async-done | bytes 3211280 | tf_op jit(solution)/shard_map/all_gather | solution.py:34
  362.8 4.2 multiply_add_fusion
  369.2 40.0 %while.106 = (s32[]{:T(128)}, f32[49,4,256]{2,1,0:T(4,128)S(1)}, f32[4,256]{1,0:T(4,128)S(1)}, f32[16,49,4,256]{3,2,1,0:T(4,128)}, f32[16,4,256]{2,1,0:T(4,128)S...) while((s32[]{:T(128)}, f32[49,4,256]{2,1,0:T(4,128)S(1)}, ...), condition=%wide.region_12.13_spmd.clone, body=%wide.region_11.12_spmd.clone.sunk | while | flops 153604 | bytes 827524 | solution.py:164
  410.8 29.8 %all_gather.46 = f32[16,4,256]{2,1,0:T(4,128)S(1)} all-gather(f32[1,4,256]{2,1,0:T(4,128)S(1)} %slice.127), channel_id=1, replica_groups=mesh['ax'=16,'rad'=4,'pit'=4] {'ax'}, dimensions={0}, use_global_device_ids=true | all-gather | bytes 69632 | tf_op jit(solution)/shard_map/all_gather | solution.py:34
  440.7 22.8 %all-gather.13.cloned.1.call-done = f32[16,49,4,256]{3,2,1,0:T(4,128)} async-done(((f32[1,49,4,256]{3,2,1,0:T(4,128)}), f32[16,49,4,256]{3,2,1,0:T(4,128)}) %all-gather.13.cloned.1.call-update) | async-done | bytes 3211280 | tf_op jit(solution)/shard_map/all_gather | solution.py:34
  463.5 14.6 %while.103 = (s32[]{:T(128)}, f32[49,4,256]{2,1,0:T(4,128)S(1)}, s32[]{:T(128)}, f32[16,4,256]{2,1,0:T(4,128)S(1)}, f32[16,49,4,256]{3,2,1,0:T(4,128)}, /*index=5*/s32[]{:T(128)}, s32[]{:T(128)}, s32[]{:T(128)}, s32[]{:T(128)}) while((s32[]{:T(128)}, f32[49,4,256]{2,1,0:T(4,128)S(1)}, s32[]{:T(128)}, f32[16,4,256]{2,1,0:T(4,128)S(1)}, ...), condition=%wide.region_14.15_spmd, body=%wide.region_13.14_spmd.sunk | while | flops 100358 | bytes 614547 | solution.py:43
  478.2 4.6 add_add_fusion
  (244 shorter events, 191.4 us)
Async XLA Ops:
  6.5 355.2 %all-gather.11.cloned.1.call-start = ((), (), s32[]{:S(2)}) async-start(), calls=%async_computation | async-start | bytes 3411968 | tf_op jit(solution)/shard_map/all_gather | solution.py:34
  8.3 175.2 %collective-permute-start = (f32[1,49,4,256]{3,2,1,0:T(4,128)}, f32[1,49,4,256]{3,2,1,0:T(4,128)S(1)}, u32[]{:S(2)}, u32[]{:S(2)}) collective-permute-start(f32[1,49,4,256]{3,2,1,0:T(4,128)} %get-tuple-element.654), channel_id=1, source_target_pairs={{0,16},{16,32},{32,48},{48,64},{64,80},{80,96},{96,112},{112,128},... | collective-permute-start | bytes 602120 | tf_op jit(solution)/shard_map/ppermute | solution.py:24
  13.2 171.1 %collective-permute-start.1 = (f32[1,49,4,256]{3,2,1,0:T(4,128)}, f32[1,49,4,256]{3,2,1,0:T(4,128)}, u32[]{:S(2)}, u32[]{:S(2)}) collective-permute-start(f32[1,49,4,256]{3,2,1,0:T(4,128)} %get-tuple-element.653), channel_id=1, source_target_pairs={{16,0},{32,16},{48,32},{64,48},{80,64},{96,80},{112,96},{128,112},... | collective-permute-start | bytes 602120 | tf_op jit(solution)/shard_map/ppermute | solution.py:25
  19.7 8.4 %copy-start.7 = (f32[3,7,7]{2,1,0:T(8,128)S(1)}, f32[3,7,7]{2,1,0:T(8,128)}, u32[]{:S(2)}) copy-start(f32[3,7,7]{2,1,0:T(8,128)} %param.18) | copy-start | bytes 1768
  19.7 9.2 %copy-start = (f32[16,49,4,256]{3,2,1,0:T(4,128)S(1)}, f32[16,49,4,256]{3,2,1,0:T(4,128)}, u32[]{:S(2)}) copy-start(f32[16,49,4,256]{3,2,1,0:T(4,128)} %param.17) | copy-start | bytes 9633796
  22.3 129.5 %collective-permute-start.4 = (f32[16,49,4,1]{1,0,3,2:T(8,128)}, f32[16,49,4,1]{1,0,3,2:T(8,128)}, u32[]{:S(2)}, u32[]{:S(2)}) collective-permute-start(f32[16,49,4,1]{1,0,3,2:T(8,128)} %copy.75), channel_id=1, source_target_pairs={{0,1},{1,2},{2,3},{3,0},{4,5},{5,6},{6,7},{7,4},{8,9},{9,10},{10,1... | collective-permute-start | bytes 37640 | tf_op jit(solution)/shard_map/ppermute | solution.py:24
  26.1 129.1 %collective-permute-start.5 = (f32[16,49,4,1]{1,0,3,2:T(8,128)}, f32[16,49,4,1]{1,0,3,2:T(8,128)}, u32[]{:S(2)}, u32[]{:S(2)}) collective-permute-start(f32[16,49,4,1]{1,0,3,2:T(8,128)} %copy.76), channel_id=1, source_target_pairs={{1,0},{2,1},{3,2},{0,3},{5,4},{6,5},{7,6},{4,7},{9,8},{10,9},{11,1... | collective-permute-start | bytes 37640 | tf_op jit(solution)/shard_map/ppermute | solution.py:25
  63.1 80.8 %copy-start.5 = (f32[16,4,256]{2,1,0:T(4,128)}, f32[16,4,256]{2,1,0:T(4,128)S(1)}, u32[]{:S(2)}) copy-start(f32[16,4,256]{2,1,0:T(4,128)S(1)} %get-tuple-element.1202) | copy-start | bytes 196612
  63.1 80.8 %copy-start.6 = (f32[16,4,256]{2,1,0:T(4,128)}, f32[16,4,256]{2,1,0:T(4,128)S(1)}, u32[]{:S(2)}) copy-start(f32[16,4,256]{2,1,0:T(4,128)S(1)} %get-tuple-element.1203) | copy-start | bytes 196612
  183.5 0.8 copy-start.4
  184.3 6.9 %copy-start.8 = (f32[3,7,7]{2,1,0:T(8,128)S(1)}, f32[3,7,7]{2,1,0:T(8,128)}, u32[]{:S(2)}) copy-start(f32[3,7,7]{2,1,0:T(8,128)} %param.18) | copy-start | bytes 1768
  186.7 22.3 %collective-permute-start.2 = (f32[18,49,1,256]{3,2,1,0:T(1,128)S(1)}, f32[18,49,1,256]{3,2,1,0:T(1,128)S(1)}, u32[]{:S(2)}, u32[]{:S(2)}) collective-permute-start(f32[18,49,1,256]{3,2,1,0:T(1,128)S(1)} %get-tuple-element.652), channel_id=1, source_target_pairs={{0,4},{4,8},{8,12},{1,5},{5,9},{9,13},{2,6},{6,10},{10,14},{3,7},{... | collective-permute-start | bytes 2709512 | tf_op jit(solution)/shard_map/ppermute | solution.py:24
  189.9 23.2 %collective-permute-start.3 = (f32[18,49,1,256]{3,2,1,0:T(1,128)S(1)}, f32[18,49,1,256]{3,2,1,0:T(1,128)S(1)}, u32[]{:S(2)}, u32[]{:S(2)}) collective-permute-start(f32[18,49,1,256]{3,2,1,0:T(1,128)S(1)} %get-tuple-element.651), channel_id=1, source_target_pairs={{4,0},{8,4},{12,8},{5,1},{9,5},{13,9},{6,2},{10,6},{14,10},{7,3},{... | collective-permute-start | bytes 2709512 | tf_op jit(solution)/shard_map/ppermute | solution.py:25
  213.2 12.5 %copy-start.1 = (f32[18,49,1,256]{3,2,1,0:T(1,128)}, f32[18,49,1,256]{3,2,1,0:T(1,128)S(1)}, u32[]{:S(2)}) copy-start(f32[18,49,1,256]{3,2,1,0:T(1,128)S(1)} %collective-permute-done.3) | copy-start | bytes 2709508
  225.8 2.2 slice-start
  225.8 2.3 slice-start.1
  243.3 2.7 copy-start.2
  307.0 156.5 %all-gather.13.cloned.1.call-start = ((), (), s32[]{:S(2)}) async-start(), calls=%async_computation.1 | async-start | bytes 3411968 | tf_op jit(solution)/shard_map/all_gather | solution.py:34
  367.0 2.1 copy-start.3
Sparse Core Ops, SparseCore 0:
  307.1 54.5 all-gather.10
  410.9 52.4 all-gather.12
where the time goes:
time: 498 us; the launch traced here: 490 us
  other arithmetic  188 us (38%)
  blocking collectives  136 us (27%)
  waiting for transfers between devices  58.9 us (12%)
  local copies, waits for them, and re-layouts  52.1 us (10%)
  matrix products  25.5 us (5%)
  starting transfers between devices  14.1 us (3%)
  between operations  13.9 us (3%)
    all_gather x6, blocking collectives, carried_in(): gathered = jax.tree.map(lambda a: lax.all_gather(a, axis), part)  136 us
    dynamic_update_slice x80, other arithmetic, on_device(): lax.scan(forward, (pivot_in, zeros_field, ones_line), (lower, upper, diag...  99.2 us
    all_gather x2, waiting for transfers between devices, carried_in(): gathered = jax.tree.map(lambda a: lax.all_gather(a, axis), part)  43.4 us
    div x34, other arithmetic, normalize(): return tuple((entry / largest for entry in mats))  33.2 us
    dot_general x3, matrix products, flux_of(): jnp.einsum('vw,nhwrp->nhvrp', matrix, by_harmonic, precision=lax.Precisio...  19.5 us
    mul x1, other arithmetic, step_rhs(): return factor[:, None] * resid  15.2 us
    add x15, other arithmetic, chain_affine(): return (later[0] * earlier[0], later[0][None] * earlier[1] + later[1])  15 us
    ppermute x3, waiting for transfers between devices, extended(): before = lax.ppermute(last, axis, up)  11.3 us
  transfers between devices with their start and end apart: 8, of which 4 were waited for; matrix products, arithmetic and copies ran while one was open for 20% of the time, Pallas kernels for 0%

commit v1 on v0

v1 whole, which is shorter than its diff:
```python
import functools

import jax
import jax.numpy as jnp
from jax import lax
from jax.experimental import pallas as pl
from jax.experimental.pallas import tpu as pltpu
from jax.sharding import PartitionSpec as P

HARM = 7
VARS = 7
HV = HARM * VARS
ROWS = 16
HALF = 25
CHUNKS = 5
PIECE = HALF // CHUNKS
MESH = pl.DeviceIdType.MESH

blade_freq = 0.6
dissipation = 0.2
courant = 1.0
section_weight = 0.5

F32 = jnp.float32
TILE = (8, 128)


def remote(src, dst, send, recv, **place):
    return pltpu.make_async_remote_copy(
        src_ref=src, dst_ref=dst, send_sem=send, recv_sem=recv, device_id=place, device_id_type=MESH
    )


def roll(x, shift, axis):
    shift = shift % x.shape[axis]
    return pltpu.roll(x, shift, axis) if shift else x


def kernel(
    sizes,
    state_hbm,
    jac,
    line,
    mask,
    out_hbm,
    st,
    bb,
    rs,
    rr,
    ps,
    pr,
    pe,
    fs,
    fr,
    am,
    dlt,
    qq,
    ww,
    zz,
    fac,
    spd,
    spk,
    ends,
    part_ends,
    x1s,
    x1r,
    bch,
    cin,
    cout,
    x2s,
    pp,
    in_sem,
    out_sem,
    a_send,
    a_recv,
    r_send,
    r_recv,
    p_send,
    p_recv,
    f_send,
    f_recv,
    e_send,
    e_recv,
    x_send,
    x_recv,
    c_send,
    c_recv,
):
    nax, nrad, npit = sizes
    chips = nax // 2
    ax = lax.axis_index("ax")
    rad = lax.axis_index("rad")
    pit = lax.axis_index("pit")
    core = lax.rem(ax, 2)
    chip = lax.div(ax, 2)
    partner = ax + 1 - 2 * core
    pit_next = lax.rem(pit + 1, npit)
    pit_prev = lax.rem(pit + npit - 1, npit)
    zero = jnp.zeros(TILE, F32)
    one = jnp.ones(TILE, F32)

    load = pltpu.make_async_copy(state_hbm, st.at[pl.ds(1, ROWS)], in_sem)
    load.start()

    barrier = pltpu.get_barrier_semaphore()

    def greet(step, carry):
        pl.semaphore_signal(
            barrier, inc=1, device_id={"ax": lax.rem(ax + step, nax)}, device_id_type=MESH
        )
        return carry

    lax.fori_loop(1, nax, greet, 0)
    pl.semaphore_signal(barrier, inc=1, device_id={"pit": pit_next}, device_id_type=MESH)
    pl.semaphore_signal(barrier, inc=1, device_id={"pit": pit_prev}, device_id_type=MESH)

    @pl.when(rad > 0)
    def _():
        pl.semaphore_signal(barrier, inc=1, device_id={"rad": rad - 1}, device_id_type=MESH)

    @pl.when(rad < nrad - 1)
    def _():
        pl.semaphore_signal(barrier, inc=1, device_id={"rad": rad + 1}, device_id_type=MESH)

    for d in range(3):
        for v in range(VARS):
            for w in range(VARS):
                am[d * 49 + v * 7 + w] = jnp.full(TILE, jac[d, v, w], F32)
    limit = zero
    for d in range(3):
        largest = zero
        for v in range(VARS):
            total = zero
            for w in range(VARS):
                total = total + jnp.abs(am[d * 49 + v * 7 + w])
            largest = jnp.maximum(largest, total)
        limit = limit + largest

    base = line[...]

    def coef_of(i):
        return base * (1.0 + mask[i].astype(F32))

    a, b, c, d_, c_prev, d_prev = one, zero, zero, one, zero, one
    for i in range(ROWS):
        inv = 1.0 / coef_of(i)
        dlt[i] = inv
        c_prev, d_prev = c, d_
        a = a + inv * c
        b = b + inv * d_
        c = a + c
        d_ = b + d_
    fs[0] = a
    fs[1] = b
    fs[2] = c_prev
    fr[ax, 0] = a
    fr[ax, 1] = b
    fr[ax, 2] = c_prev

    for side, edge in ((0, 0), (1, nrad - 1)):

        @pl.when(rad == edge)
        def _():
            def clear(h, carry):
                for g in range(4):
                    for v in range(VARS):
                        rr[side, h, g, v] = zero
                return carry

            lax.fori_loop(0, HARM, clear, 0)

    @pl.when(ax == 0)
    def _():
        def clear(c, carry):
            st[0, c] = zero
            return carry

        lax.fori_loop(0, HV, clear, 0)

    @pl.when(ax == nax - 1)
    def _():
        def clear(c, carry):
            st[ROWS + 1, c] = zero
            return carry

        lax.fori_loop(0, HV, clear, 0)

    @pl.when(chip == 0)
    def _():
        for k in range(HALF):
            cin[0, k] = zero

    @pl.when(chip == chips - 1)
    def _():
        for k in range(HALF):
            cin[1, k] = zero

    for t in range(2):
        x1s[t, HV] = zero

    radial_peers = jnp.minimum(rad, 1) + jnp.minimum(nrad - 1 - rad, 1)
    pl.semaphore_wait(barrier, nax - 1 + 2 + radial_peers)
    load.wait()

    def axial_up(peer):
        return remote(st.at[ROWS], st.at[0], a_send.at[0], a_recv.at[0], ax=peer)

    def axial_down(peer):
        return remote(st.at[1], st.at[ROWS + 1], a_send.at[1], a_recv.at[1], ax=peer)

    sub = lax.broadcasted_iota(jnp.int32, TILE, 0)
    lane = lax.broadcasted_iota(jnp.int32, TILE, 1)
    row = lax.rem(sub, 4)
    is_row = [row == j for j in range(4)]

    def packed(g, c):
        rows = [st[1 + 4 * g + j, c] for j in range(4)]
        up = rows[3]
        down = rows[0]
        for j in range(3):
            up = jnp.where(is_row[j], roll(rows[j], j - 3, 0), up)
        for j in range(1, 4):
            down = jnp.where(is_row[j], roll(rows[j], j, 0), down)
        return up, down

    def speed_of(x):
        return 1.0 + 0.5 * jnp.tanh(x)

    for g in range(4):
        up, down = packed(g, 0)
        spk[0, g] = speed_of(up)
        spk[1, g] = speed_of(down)

    def radial_up(h, peer):
        return remote(rs.at[0, h], rr.at[0, h], r_send.at[0, h], r_recv.at[0, h], rad=peer)

    def radial_down(h, peer):
        return remote(rs.at[1, h], rr.at[1, h], r_send.at[1, h], r_recv.at[1, h], rad=peer)

    def radial(h, carry):
        def group(g, carry):
            su, sd = spk[0, g], spk[1, g]
            ups, downs, wups, wdowns = [], [], [], []
            for v in range(VARS):
                up, down = packed(g, h * VARS + v)
                ups.append(up)
                downs.append(down)
                wups.append(su * up)
                wdowns.append(sd * down)
            for v in range(VARS):
                tu = -2.0 * dissipation * ups[v]
                td = -2.0 * dissipation * downs[v]
                for w in range(VARS):
                    m = am[49 + v * 7 + w]
                    tu = tu - m * wups[w]
                    td = td + m * wdowns[w]
                rs[0, h, g, v] = tu
                rs[1, h, g, v] = td
            return carry

        lax.fori_loop(0, 4, group, 0)

        @pl.when(rad < nrad - 1)
        def _():
            radial_up(h, rad + 1).start()

        @pl.when(rad > 0)
        def _():
            radial_down(h, rad - 1).start()

        return carry

    lax.fori_loop(0, HARM, radial, 0)

    @pl.when(ax < nax - 1)
    def _():
        axial_up(ax + 1).start()

    @pl.when(ax > 0)
    def _():
        axial_down(ax - 1).start()

    def factor(step):
        return remote(
            fs, fr.at[ax], f_send.at[step], f_recv.at[ax], ax=lax.rem(ax + step, nax)
        )

    def send_factor(step, carry):
        factor(step).start()
        return carry

    lax.fori_loop(1, nax, send_factor, 0)

    pair = lax.div(lane, 2)

    def pack(i, carry):
        got = zero
        for c in range(HV):
            got = jnp.where(pair == c, roll(st[1 + i, c], 2 * c + 1, 1), got)
        ps[i] = got
        return carry

    lax.fori_loop(0, ROWS, pack, 0)
    pitch_next = remote(ps, pr.at[0], p_send.at[0], p_recv.at[0], pit=pit_next)
    pitch_prev = remote(ps, pr.at[1], p_send.at[1], p_recv.at[1], pit=pit_prev)
    pitch_next.start()
    pitch_prev.start()

    def tables(i, carry):
        s = speed_of(st[1 + i, 0])
        spd[1 + i] = s
        coef = coef_of(i)
        radius = s * limit + (6.0 * dissipation + HARM // 2 * blade_freq)
        fac[i] = (-0.5 * section_weight * courant) * jnp.sqrt(1.0 + 4.0 * coef) / (coef * radius)
        return carry

    lax.fori_loop(0, ROWS, tables, 0)

    pitch_next.wait_recv()
    pitch_prev.wait_recv()
    top = sub >= 4
    even = lax.rem(lane, 2) == 0

    def merge(i, carry):
        own = ps[i]
        before = jnp.where(top, pr[0, i], own)
        after = jnp.where(top, own, pr[1, i])
        both = jnp.where(even, roll(after, -1, 1), roll(before, 1, 1))
        pe[i] = roll(both, 4, 0)
        return carry

    lax.fori_loop(0, ROWS, merge, 0)

    @pl.when(ax > 0)
    def _():
        axial_up(ax - 1).wait_recv()

    @pl.when(ax < nax - 1)
    def _():
        axial_down(ax + 1).wait_recv()

    spd[0] = speed_of(st[0, 0])
    spd[ROWS + 1] = speed_of(st[ROWS + 1, 0])

    first_lane = lane == 0
    last_lane = lane == 127
    inner_low = row > 0
    inner_high = row < 3

    def sides(i, carry):
        pitched = pe[i]
        sa, sc, sb = spd[i], spd[1 + i], spd[2 + i]
        su = roll(sc, 1, 0)
        sd = roll(sc, -1, 0)
        scale = fac[i]
        sl = sr = None
        middle = []
        accs = []
        for h in range(HARM):
            d0, d1, d2, acc = [], [], [], []
            for v in range(VARS):
                c = h * VARS + v
                here, back, ahead = st[1 + i, c], st[i, c], st[2 + i, c]
                e = roll(pitched, -(2 * c + 1), 1)
                left = jnp.where(first_lane, e, roll(here, 1, 1))
                right = jnp.where(last_lane, e, roll(here, -1, 1))
                if c == 0:
                    sl, sr = speed_of(left), speed_of(right)
                under = jnp.where(inner_low, roll(here, 1, 0), 0.0)
                over = jnp.where(inner_high, roll(here, -1, 0), 0.0)
                d0.append(sb * ahead - sa * back)
                d1.append(sd * over - su * under)
                d2.append(sr * right - sl * left)
                around = ((back + ahead) + (left + right)) + (under + over)
                acc.append(12.0 * dissipation * here - 2.0 * dissipation * around)
                if h:
                    k = (h + 1) // 2
                    twin = st[1 + i, c + VARS if h % 2 else c - VARS]
                    sign = 2.0 * k * blade_freq if h % 2 else -2.0 * k * blade_freq
                    acc[v] = acc[v] + sign * twin
            for v in range(VARS):
                t = acc[v]
                for w in range(VARS):
                    t = t + am[v * 7 + w] * d0[w]
                    t = t + am[49 + v * 7 + w] * d1[w]
                    t = t + am[98 + v * 7 + w] * d2[w]
                bb[i, h * VARS + v] = scale * t
        return carry

    lax.fori_loop(0, ROWS, sides, 0)

    def arrive(step, carry):
        source = lax.rem(ax + nax - step, nax)
        remote(fs, fr.at[source], f_send.at[step], f_recv.at[source], ax=source).wait_recv()
        return carry

    lax.fori_loop(1, nax, arrive, 0)

    def entries(j):
        a, b, c_prev = fr[j, 0], fr[j, 1], fr[j, 2]
        return a, b, c_prev, (1.0 + b * c_prev) / a

    def ahead_of(j, carry):
        n, m = carry
        a, b, c_prev, d_prev = entries(j)
        return a * n + b * m, (a + c_prev) * n + (b + d_prev) * m

    n, m = lax.fori_loop(0, ax, ahead_of, (one, one))
    e_in = n / m

    def behind(t, carry):
        n, m = carry
        a, b, c_prev, d_prev = entries(nax - 1 - t)
        return d_prev * n + b * m, (c_prev + d_prev) * n + (a + b) * m

    n, m = lax.fori_loop(0, nax - 1 - ax, behind, (one, one))
    f_in = n / m

    e = e_in
    run = one
    for i in range(ROWS):
        t = dlt[i] + e
        q = 1.0 / (1.0 + t)
        e = t * q
        run = run * q
        qq[i] = q
        ww[i] = run
    f = f_in
    for i in reversed(range(ROWS)):
        t = dlt[i] + f
        s = 1.0 / (1.0 + t)
        f = t * s
        zz[i] = s
    back_run = one
    for i in range(ROWS):
        back_run = back_run * zz[i]
        zz[i] = back_run
    ends[0] = run
    ends[1] = back_run
    ends[2] = 1.0 - f_in
    ends[3] = e + f_in * qq[ROWS - 1]
    send_ends = remote(ends.at[pl.ds(0, 2)], part_ends, e_send, e_recv, ax=partner)
    send_ends.start()

    edge_low = is_row[0]
    edge_high = is_row[3]

    def eliminate(h, carry):
        @pl.when(rad > 0)
        def _():
            radial_up(h, rad - 1).wait_recv()

        @pl.when(rad < nrad - 1)
        def _():
            radial_down(h, rad + 1).wait_recv()

        def group(g, carry):
            carried, sums = list(carry[0]), list(carry[1])
            for j in range(4):
                i = 4 * g + j
                scale, q, z = fac[i], qq[i], zz[i]
                for v in range(VARS):
                    low = roll(rr[0, h, g, v], -j, 0)
                    high = roll(rr[1, h, g, v], 3 - j, 0)
                    extra = jnp.where(edge_low, low, jnp.where(edge_high, high, 0.0))
                    right = bb[i, h * VARS + v] + scale * extra
                    carried[v] = q * (right + carried[v])
                    sums[v] = sums[v] + z * right
                    bb[i, h * VARS + v] = carried[v]
            return tuple(carried), tuple(sums)

        zeros = (zero,) * VARS
        carried, sums = lax.fori_loop(0, 4, group, (zeros, zeros))
        for v in range(VARS):
            x1s[0, h * VARS + v] = carried[v]
            x1s[1, h * VARS + v] = sums[v]
        return carry

    lax.fori_loop(0, HARM, eliminate, 0)

    mine = core * HALF
    theirs = HALF - mine
    swap = remote(
        x1s.at[:, pl.ds(theirs, HALF)], x1r, x_send.at[0], x_recv.at[0], ax=partner
    )
    swap.start()
    send_ends.wait_recv()
    lower = core == 0
    alpha0 = jnp.where(lower, ends[0], part_ends[0])
    alpha1 = jnp.where(lower, part_ends[0], ends[0])
    gamma0 = jnp.where(lower, ends[1], part_ends[1])
    gamma1 = jnp.where(lower, part_ends[1], ends[1])
    through = (alpha0 * alpha1, gamma0 * gamma1)
    swap.wait_recv()

    def pair_values(t, k):
        own, other = x1s[t, mine + k], x1r[t, k]
        return jnp.where(lower, own, other), jnp.where(lower, other, own)

    for k in range(HALF):
        b0, b1 = pair_values(0, k)
        bch[0, k] = alpha1 * b0 + b1
        g0, g1 = pair_values(1, k)
        bch[1, k] = gamma0 * g1 + g0

    second_half = lax.div(2 * chip, chips)

    def chain_copy(t, k, peer):
        return remote(
            cout.at[t, pl.ds(k * PIECE, PIECE)],
            cin.at[t, pl.ds(k * PIECE, PIECE)],
            c_send.at[t, k],
            c_recv.at[t, k],
            ax=peer,
        )

    def sends(t):
        to = chip + 1 - 2 * t
        return (to >= 0) & (to < chips)

    def receives(t):
        source = chip - 1 + 2 * t
        return (source >= 0) & (source < chips)

    def direction(turn, carry):
        t = lax.rem(second_half + turn, 2)
        factor_of = jnp.where(t == 0, through[0], through[1])

        def piece(k, carry):
            @pl.when(receives(t))
            def _():
                chain_copy(t, k, ax - 2 + 4 * t).wait_recv()

            @pl.when(sends(t))
            def _():
                for m in range(PIECE):
                    at = k * PIECE + m
                    cout[t, at] = factor_of * cin[t, at] + bch[t, at]
                chain_copy(t, k, ax + 2 - 4 * t).start()

            return carry

        lax.fori_loop(0, CHUNKS, piece, 0)
        return carry

    lax.fori_loop(0, 2, direction, 0)

    for k in range(HALF):
        p, r = cin[0, k], cin[1, k]
        b0, b1 = pair_values(0, k)
        g0, g1 = pair_values(1, k)
        p1 = alpha0 * p + b0
        r0 = gamma1 * r + g1
        pp[0, mine + k] = jnp.where(lower, p, p1)
        pp[1, mine + k] = jnp.where(lower, r0, r)
        x2s[0, k] = jnp.where(lower, p1, p)
        x2s[1, k] = jnp.where(lower, r, r0)
    back = remote(
        x2s, pp.at[:, pl.ds(mine, HALF)], x_send.at[1], x_recv.at[1], ax=partner
    )
    back.start()
    back_in = remote(
        x2s, pp.at[:, pl.ds(theirs, HALF)], x_send.at[1], x_recv.at[1], ax=partner
    )
    back_in.wait_recv()

    def finish_copy(h):
        part = pl.ds(h * VARS, VARS)
        return pltpu.make_async_copy(bb.at[:, part], out_hbm.at[:, part], out_sem.at[h])

    def finish(h, carry):
        entering, after = [], []
        for v in range(VARS):
            c = h * VARS + v
            p = pp[0, c]
            whole = ends[0] * p + x1s[0, c]
            entering.append(p)
            after.append((pp[1, c] + ends[2] * whole) / ends[3])

        def back_row(t, after):
            i = ROWS - 1 - t
            q, w = qq[i], ww[i]
            following = []
            for v in range(VARS):
                c = h * VARS + v
                x = (bb[i, c] + w * entering[v]) + q * after[v]
                following.append(x)
                bb[i, c] = st[1 + i, c] + x
            return tuple(following)

        lax.fori_loop(0, ROWS, back_row, tuple(after))
        finish_copy(h).start()
        return carry

    lax.fori_loop(0, HARM, finish, 0)

    @pl.when(ax < nax - 1)
    def _():
        axial_up(ax + 1).wait_send()

    @pl.when(ax > 0)
    def _():
        axial_down(ax - 1).wait_send()

    def sent(step, carry):
        factor(step).wait_send()
        return carry

    lax.fori_loop(1, nax, sent, 0)
    pitch_next.wait_send()
    pitch_prev.wait_send()
    send_ends.wait_send()
    swap.wait_send()
    back.wait_send()

    def sent_radial(h, carry):
        @pl.when(rad < nrad - 1)
        def _():
            radial_up(h, rad + 1).wait_send()

        @pl.when(rad > 0)
        def _():
            radial_down(h, rad - 1).wait_send()

        return carry

    lax.fori_loop(0, HARM, sent_radial, 0)

    for t in range(2):

        @pl.when(sends(t))
        def _():
            def sent_piece(k, carry):
                chain_copy(t, k, ax + 2 - 4 * t).wait_send()
                return carry

            lax.fori_loop(0, CHUNKS, sent_piece, 0)

    def written(h, carry):
        finish_copy(h).wait()
        return carry

    lax.fori_loop(0, HARM, written, 0)


def solution(mesh):
    sizes = (mesh.shape["ax"], mesh.shape["rad"], mesh.shape["pit"])
    nax = sizes[0]

    def to_tiles(x):
        lead = x.shape[:-2]
        x = x.reshape(lead + (4, 2, 128))
        n = len(lead)
        x = x.transpose(tuple(range(n)) + (n + 1, n, n + 2))
        return x.reshape(lead + TILE)

    def from_tiles(x):
        lead = x.shape[:-2]
        x = x.reshape(lead + (2, 4, 128))
        n = len(lead)
        x = x.transpose(tuple(range(n)) + (n + 1, n, n + 2))
        return x.reshape(lead + (4, 256))

    def vmem(*lead):
        return pltpu.VMEM(lead + TILE, F32)

    dma = pltpu.SemaphoreType.DMA

    def on_device(state, flux_jac, line_coef, line_mask):
        out = pl.pallas_call(
            functools.partial(kernel, sizes),
            out_shape=jax.ShapeDtypeStruct((ROWS, HV) + TILE, F32),
            in_specs=[
                pl.BlockSpec(memory_space=pl.ANY),
                pl.BlockSpec(memory_space=pltpu.SMEM),
                pl.BlockSpec(memory_space=pltpu.VMEM),
                pl.BlockSpec(memory_space=pltpu.VMEM),
            ],
            out_specs=pl.BlockSpec(memory_space=pl.ANY),
            scratch_shapes=[
                vmem(ROWS + 2, HV),
                vmem(ROWS, HV),
                vmem(2, HARM, 4, VARS),
                vmem(2, HARM, 4, VARS),
                vmem(ROWS),
                vmem(2, ROWS),
                vmem(ROWS),
                vmem(3),
                vmem(nax, 3),
                vmem(3 * VARS * VARS),
                vmem(ROWS),
                vmem(ROWS),
                vmem(ROWS),
                vmem(ROWS),
                vmem(ROWS),
                vmem(ROWS + 2),
                vmem(2, 4),
                vmem(4),
                vmem(2),
                vmem(2, 2 * HALF),
                vmem(2, HALF),
                vmem(2, HALF),
                vmem(2, HALF),
                vmem(2, HALF),
                vmem(2, HALF),
                vmem(2, 2 * HALF),
                dma,
                dma((HARM,)),
                dma((2,)),
                dma((2,)),
                dma((2, HARM)),
                dma((2, HARM)),
                dma((2,)),
                dma((2,)),
                dma((nax,)),
                dma((nax,)),
                dma,
                dma,
                dma((2,)),
                dma((2,)),
                dma((2, CHUNKS)),
                dma((2, CHUNKS)),
            ],
            compiler_params=pltpu.CompilerParams(
                collective_id=0, has_side_effects=True, vmem_limit_bytes=40 * 1024 * 1024
            ),
        )(to_tiles(state), flux_jac, to_tiles(line_coef), to_tiles(line_mask))
        return from_tiles(out)

    return jax.shard_map(
        on_device,
        mesh=mesh,
        in_specs=(P("ax", None, "rad", "pit"), P(), P("rad", "pit"), P("ax", "rad", "pit")),
        out_specs=P("ax", None, "rad", "pit"),
        check_vma=False,
    )
```

time: 498 us -> 61.2 us (0.12); the launches traced: 490 us -> 61 us
  other arithmetic: 188 us -> 0 us
  blocking collectives: 136 us -> 0 us
  waiting for transfers between devices: 58.9 us -> 0 us
  Pallas kernels: 0 us -> 55.2 us
  local copies, waits for them, and re-layouts: 52.1 us -> 5.83 us
  matrix products: 25.5 us -> 0 us
  starting transfers between devices: 14.1 us -> 0 us
  between operations: 13.9 us -> 0.01 us
    all_gather x6 -> x0, blocking collectives: 136 us -> none  [carried_in(): gathered = jax.tree.map(lambda a: lax.all_gather(a, axis), part)]
    dynamic_update_slice x80 -> x0, other arithmetic: 99.2 us -> none  [on_device(): lax.scan(forward, (pivot_in, zeros_field, ones_line), (lower, upper, diag...]
    pallas_call x0 -> x1, Pallas kernels: none -> 55.2 us  [on_device(): pl.pallas_call(functools.partial(kernel, sizes), out_shape=jax.ShapeDtype...]
    all_gather x2 -> x0, waiting for transfers between devices: 43.4 us -> none  [carried_in(): gathered = jax.tree.map(lambda a: lax.all_gather(a, axis), part)]
    div x36 -> x0, other arithmetic: 35.4 us -> none  [the longest x34 33.2 us: normalize(): return tuple((entry / largest for entry in mats))]
    dot_general x4 -> x0, matrix products: 25.5 us -> none  [the longest x3 19.5 us: flux_of(): jnp.einsum('vw,nhwrp->nhvrp', matrix, by_harmonic, precision=lax.Precisio...]
    add x17 -> x0, other arithmetic: 23.8 us -> none  [the longest x15 15 us: chain_affine(): return (later[0] * earlier[0], later[0][None] * earlier[1] + later[1])]
    mul x7 -> x0, other arithmetic: 20.6 us -> none  [the longest x1 15.2 us: step_rhs(): return factor[:, None] * resid]
  transfers between devices with their start and end apart: 8 -> 0, of which waited for: 4 -> 0; matrix products, arithmetic and copies ran while one was open for 20% -> 0% of each run, Pallas kernels for 0% -> 0%
where the time goes in v1:
time: 61.2 us; the launch traced here: 61 us
  Pallas kernels  55.2 us (90%)
  local copies, waits for them, and re-layouts  5.83 us (10%)
    pallas_call x1, Pallas kernels, on_device(): pl.pallas_call(functools.partial(kernel, sizes), out_shape=jax.ShapeDtype...  55.2 us
    unnamed x9, local copies, waits for them, and re-layouts  5.83 us

profile of v1, /device:TPU:1, one launch (start us, length us, event | category | flops | bytes accessed | tf_op | source)
XLA Modules:
  0.0 61.0 jit_solution(9113292850769249803)
XLA Ops:
  0.0 0.0 copy-start
  0.0 1.9 %copy-done = f32[16,49,4,256]{3,2,1,0:T(4,128)S(1)} copy-done((f32[16,49,4,256]{3,2,1,0:T(4,128)S(1)}, f32[16,49,4,256]{3,2,1,0:T(4,128)}, u32[]{:S(2)}) %copy-start) | copy-done | bytes 3211288
  1.9 0.0 copy-start.1
  1.9 0.8 %copy-done.1 = s32[16,4,256]{2,1,0:T(4,128)S(1)} copy-done((s32[16,4,256]{2,1,0:T(4,128)S(1)}, s32[16,4,256]{2,1,0:T(4,128)}, u32[]{:S(2)}) %copy-start.1) | copy-done | bytes 65560
  2.7 0.0 copy-start.2
  2.8 0.7 %copy-done.2 = f32[3,7,7]{2,1,0:T(8,128)S(1)} copy-done((f32[3,7,7]{2,1,0:T(8,128)S(1)}, f32[3,7,7]{2,1,0:T(8,128)}, u32[]{:S(2)}) %copy-start.2) | copy-done | bytes 612
  3.5 0.0 copy-start.3
  3.5 0.7 %copy-done.3 = f32[4,256]{1,0:T(4,128)S(1)} copy-done((f32[4,256]{1,0:T(4,128)S(1)}, f32[4,256]{1,0:T(4,128)}, u32[]{:S(2)}) %copy-start.3) | copy-done | bytes 4120
  4.1 55.2 %shard_map.46 = f32[16,49,8,128]{3,2,1,0:T(8,128)S(1)} custom-call(f32[16,49,8,128]{3,2,1,0:T(8,128)S(1)} %bitcast.21, f32[3,7,7]{2,1,0:T(8,128)S(1)} %copy-done.2, f32[8,128]{1,0:T(8,128)S(1)} %bitcast.23, s32[16,8,128]{2,1,0:T(8,128)S(1)} %bitcast.22), custom_call_target="tpu_custom_call" | custom-call | tf_op jit(solution)/shard_map/pallas_call | solution.py:670
  59.3 1.7 %copy.10 = f32[16,49,4,256]{3,2,1,0:T(4,128)} copy(f32[16,49,4,256]{3,2,1,0:T(4,128)S(1)} %bitcast.20) | data formatting | bytes 6422528
Async XLA Ops:
  0.0 1.9 %copy-start = (f32[16,49,4,256]{3,2,1,0:T(4,128)S(1)}, f32[16,49,4,256]{3,2,1,0:T(4,128)}, u32[]{:S(2)}) copy-start(f32[16,49,4,256]{3,2,1,0:T(4,128)} %param.4) | copy-start | bytes 9633796
  1.9 0.8 %copy-start.1 = (s32[16,4,256]{2,1,0:T(4,128)S(1)}, s32[16,4,256]{2,1,0:T(4,128)}, u32[]{:S(2)}) copy-start(s32[16,4,256]{2,1,0:T(4,128)} %param.7) | copy-start | bytes 196612
  2.7 0.7 %copy-start.2 = (f32[3,7,7]{2,1,0:T(8,128)S(1)}, f32[3,7,7]{2,1,0:T(8,128)}, u32[]{:S(2)}) copy-start(f32[3,7,7]{2,1,0:T(8,128)} %jac.1) | copy-start | bytes 1768
  3.5 0.7 %copy-start.3 = (f32[4,256]{1,0:T(4,128)S(1)}, f32[4,256]{1,0:T(4,128)}, u32[]{:S(2)}) copy-start(f32[4,256]{1,0:T(4,128)} %param.6) | copy-start | bytes 12292

commit v2 on v1

--- a/solution.py
+++ b/solution.py
@@ -11,9 +11,6 @@
 VARS = 7
 HV = HARM * VARS
 ROWS = 16
-HALF = 25
-CHUNKS = 5
-PIECE = HALF // CHUNKS
 MESH = pl.DeviceIdType.MESH
 
 blade_freq = 0.6
@@ -39,10 +36,13 @@
 def kernel(
     sizes,
     state_hbm,
+    jac_hbm,
+    line_hbm,
+    mask_hbm,
+    out_hbm,
     jac,
     line,
     mask,
-    out_hbm,
     st,
     bb,
     rs,
@@ -64,11 +64,10 @@
     part_ends,
     x1s,
     x1r,
-    bch,
     cin,
     cout,
     x2s,
-    pp,
+    x2r,
     in_sem,
     out_sem,
     a_send,
@@ -81,8 +80,10 @@
     f_recv,
     e_send,
     e_recv,
-    x_send,
-    x_recv,
+    s_send,
+    s_recv,
+    b_send,
+    b_recv,
     c_send,
     c_recv,
 ):
@@ -99,8 +100,14 @@
     zero = jnp.zeros(TILE, F32)
     one = jnp.ones(TILE, F32)
 
-    load = pltpu.make_async_copy(state_hbm, st.at[pl.ds(1, ROWS)], in_sem)
+    load = pltpu.make_async_copy(state_hbm, st.at[pl.ds(1, ROWS)], in_sem.at[0])
     load.start()
+    load_jac = pltpu.make_async_copy(jac_hbm, jac, in_sem.at[1])
+    load_jac.start()
+    load_line = pltpu.make_async_copy(line_hbm, line, in_sem.at[2])
+    load_line.start()
+    load_mask = pltpu.make_async_copy(mask_hbm, mask, in_sem.at[3])
+    load_mask.start()
 
     barrier = pltpu.get_barrier_semaphore()
 
@@ -122,6 +129,7 @@
     def _():
         pl.semaphore_signal(barrier, inc=1, device_id={"rad": rad + 1}, device_id_type=MESH)
 
+    load_jac.wait()
     for d in range(3):
         for v in range(VARS):
             for w in range(VARS):
@@ -136,6 +144,8 @@
             largest = jnp.maximum(largest, total)
         limit = limit + largest
 
+    load_line.wait()
+    load_mask.wait()
     base = line[...]
 
     def coef_of(i):
@@ -153,9 +163,7 @@
     fs[0] = a
     fs[1] = b
     fs[2] = c_prev
-    fr[ax, 0] = a
-    fr[ax, 1] = b
-    fr[ax, 2] = c_prev
+    fs[3] = d_prev
 
     for side, edge in ((0, 0), (1, nrad - 1)):
 
@@ -185,21 +193,17 @@
 
         lax.fori_loop(0, HV, clear, 0)
 
-    @pl.when(chip == 0)
-    def _():
-        for k in range(HALF):
-            cin[0, k] = zero
-
-    @pl.when(chip == chips - 1)
-    def _():
-        for k in range(HALF):
-            cin[1, k] = zero
-
-    for t in range(2):
-        x1s[t, HV] = zero
-
-    radial_peers = jnp.minimum(rad, 1) + jnp.minimum(nrad - 1 - rad, 1)
-    pl.semaphore_wait(barrier, nax - 1 + 2 + radial_peers)
+    far = jnp.where(core == 0, chip, chips - 1 - chip)
+    passes = far < chips - 1
+    gets = far > 0
+    chain_to = ax + 2 - 4 * core
+    chain_from = ax - 2 + 4 * core
+
+    @pl.when(far == 0)
+    def _():
+        for c in range(HV):
+            cin[c] = zero
+
     load.wait()
 
     def axial_up(peer):
@@ -210,6 +214,20 @@
 
     sub = lax.broadcasted_iota(jnp.int32, TILE, 0)
     lane = lax.broadcasted_iota(jnp.int32, TILE, 1)
+
+    pair = lax.div(lane, 2)
+
+    def pack(i, carry):
+        got = zero
+        for c in range(HV):
+            got = jnp.where(pair == c, roll(st[1 + i, c], 2 * c + 1, 1), got)
+        ps[i] = got
+        return carry
+
+    lax.fori_loop(0, ROWS, pack, 0)
+    pitch_next = remote(ps, pr.at[0], p_send.at[0], p_recv.at[0], pit=pit_next)
+    pitch_prev = remote(ps, pr.at[1], p_send.at[1], p_recv.at[1], pit=pit_prev)
+
     row = lax.rem(sub, 4)
     is_row = [row == j for j in range(4)]
 
@@ -260,51 +278,14 @@
 
         lax.fori_loop(0, 4, group, 0)
 
-        @pl.when(rad < nrad - 1)
-        def _():
-            radial_up(h, rad + 1).start()
-
-        @pl.when(rad > 0)
-        def _():
-            radial_down(h, rad - 1).start()
-
         return carry
 
     lax.fori_loop(0, HARM, radial, 0)
-
-    @pl.when(ax < nax - 1)
-    def _():
-        axial_up(ax + 1).start()
-
-    @pl.when(ax > 0)
-    def _():
-        axial_down(ax - 1).start()
 
     def factor(step):
         return remote(
             fs, fr.at[ax], f_send.at[step], f_recv.at[ax], ax=lax.rem(ax + step, nax)
         )
-
-    def send_factor(step, carry):
-        factor(step).start()
-        return carry
-
-    lax.fori_loop(1, nax, send_factor, 0)
-
-    pair = lax.div(lane, 2)
-
-    def pack(i, carry):
-        got = zero
-        for c in range(HV):
-            got = jnp.where(pair == c, roll(st[1 + i, c], 2 * c + 1, 1), got)
-        ps[i] = got
-        return carry
-
-    lax.fori_loop(0, ROWS, pack, 0)
-    pitch_next = remote(ps, pr.at[0], p_send.at[0], p_recv.at[0], pit=pit_next)
-    pitch_prev = remote(ps, pr.at[1], p_send.at[1], p_recv.at[1], pit=pit_prev)
-    pitch_next.start()
-    pitch_prev.start()
 
     def tables(i, carry):
         s = speed_of(st[1 + i, 0])
@@ -316,6 +297,39 @@
 
     lax.fori_loop(0, ROWS, tables, 0)
 
+    radial_peers = jnp.minimum(rad, 1) + jnp.minimum(nrad - 1 - rad, 1)
+    pl.semaphore_wait(barrier, nax - 1 + 2 + radial_peers)
+    pitch_next.start()
+    pitch_prev.start()
+
+    @pl.when(ax < nax - 1)
+    def _():
+        axial_up(ax + 1).start()
+
+    @pl.when(ax > 0)
+    def _():
+        axial_down(ax - 1).start()
+
+    def send_radial(h, carry):
+        @pl.when(rad < nrad - 1)
+        def _():
+            radial_up(h, rad + 1).start()
+
+        @pl.when(rad > 0)
+        def _():
+            radial_down(h, rad - 1).start()
+
+        return carry
+
+    lax.fori_loop(0, HARM, send_radial, 0)
+
+    def send_factor(step, carry):
+        factor(step).start()
+        return carry
+
+    lax.fori_loop(1, nax, send_factor, 0)
+
+
     pitch_next.wait_recv()
     pitch_prev.wait_recv()
     top = sub >= 4
@@ -331,23 +345,26 @@
 
     lax.fori_loop(0, ROWS, merge, 0)
 
-    @pl.when(ax > 0)
-    def _():
-        axial_up(ax - 1).wait_recv()
-
-    @pl.when(ax < nax - 1)
-    def _():
-        axial_down(ax + 1).wait_recv()
-
-    spd[0] = speed_of(st[0, 0])
-    spd[ROWS + 1] = speed_of(st[ROWS + 1, 0])
-
     first_lane = lane == 0
     last_lane = lane == 127
     inner_low = row > 0
     inner_high = row < 3
 
-    def sides(i, carry):
+    def sides(step, carry):
+        @pl.when(step == ROWS - 2)
+        def _():
+            @pl.when(ax > 0)
+            def _():
+                axial_up(ax - 1).wait_recv()
+
+            @pl.when(ax < nax - 1)
+            def _():
+                axial_down(ax + 1).wait_recv()
+
+            spd[0] = speed_of(st[0, 0])
+            spd[ROWS + 1] = speed_of(st[ROWS + 1, 0])
+
+        i = lax.rem(step + 1, ROWS)
         pitched = pe[i]
         sa, sc, sb = spd[i], spd[1 + i], spd[2 + i]
         su = roll(sc, 1, 0)
@@ -397,8 +414,7 @@
     lax.fori_loop(1, nax, arrive, 0)
 
     def entries(j):
-        a, b, c_prev = fr[j, 0], fr[j, 1], fr[j, 2]
-        return a, b, c_prev, (1.0 + b * c_prev) / a
+        return fr[j, 0], fr[j, 1], fr[j, 2], fr[j, 3]
 
     def ahead_of(j, carry):
         n, m = carry
@@ -416,29 +432,28 @@
     n, m = lax.fori_loop(0, nax - 1 - ax, behind, (one, one))
     f_in = n / m
 
-    e = e_in
-    run = one
+    n, m = e_in, one
     for i in range(ROWS):
-        t = dlt[i] + e
-        q = 1.0 / (1.0 + t)
-        e = t * q
-        run = run * q
-        qq[i] = q
-        ww[i] = run
-    f = f_in
+        n = n + dlt[i] * m
+        after = n + m
+        inv = 1.0 / after
+        qq[i] = m * inv
+        ww[i] = inv
+        m = after
+    e_out = n * inv
+    n, m = f_in, one
+    values = []
     for i in reversed(range(ROWS)):
-        t = dlt[i] + f
-        s = 1.0 / (1.0 + t)
-        f = t * s
-        zz[i] = s
-    back_run = one
-    for i in range(ROWS):
-        back_run = back_run * zz[i]
-        zz[i] = back_run
-    ends[0] = run
-    ends[1] = back_run
+        values.append((i, m))
+        n = n + dlt[i] * m
+        m = n + m
+    inv = 1.0 / m
+    for i, value in values:
+        zz[i] = value * inv
+    ends[0] = ww[ROWS - 1]
+    ends[1] = inv
     ends[2] = 1.0 - f_in
-    ends[3] = e + f_in * qq[ROWS - 1]
+    ends[3] = 1.0 / (e_out + f_in * qq[ROWS - 1])
     send_ends = remote(ends.at[pl.ds(0, 2)], part_ends, e_send, e_recv, ax=partner)
     send_ends.start()
 
@@ -476,106 +491,76 @@
             x1s[1, h * VARS + v] = sums[v]
         return carry
 
-    lax.fori_loop(0, HARM, eliminate, 0)
-
-    mine = core * HALF
-    theirs = HALF - mine
-    swap = remote(
-        x1s.at[:, pl.ds(theirs, HALF)], x1r, x_send.at[0], x_recv.at[0], ax=partner
-    )
-    swap.start()
-    send_ends.wait_recv()
     lower = core == 0
-    alpha0 = jnp.where(lower, ends[0], part_ends[0])
-    alpha1 = jnp.where(lower, part_ends[0], ends[0])
-    gamma0 = jnp.where(lower, ends[1], part_ends[1])
-    gamma1 = jnp.where(lower, part_ends[1], ends[1])
-    through = (alpha0 * alpha1, gamma0 * gamma1)
-    swap.wait_recv()
-
-    def pair_values(t, k):
-        own, other = x1s[t, mine + k], x1r[t, k]
-        return jnp.where(lower, own, other), jnp.where(lower, other, own)
-
-    for k in range(HALF):
-        b0, b1 = pair_values(0, k)
-        bch[0, k] = alpha1 * b0 + b1
-        g0, g1 = pair_values(1, k)
-        bch[1, k] = gamma0 * g1 + g0
-
-    second_half = lax.div(2 * chip, chips)
-
-    def chain_copy(t, k, peer):
+
+    def piece(h):
+        return pl.ds(h * VARS, VARS)
+
+    def swap(h):
         return remote(
-            cout.at[t, pl.ds(k * PIECE, PIECE)],
-            cin.at[t, pl.ds(k * PIECE, PIECE)],
-            c_send.at[t, k],
-            c_recv.at[t, k],
-            ax=peer,
+            x1s.at[1 - core, piece(h)], x1r.at[piece(h)], s_send.at[h], s_recv.at[h], ax=partner
         )
 
-    def sends(t):
-        to = chip + 1 - 2 * t
-        return (to >= 0) & (to < chips)
-
-    def receives(t):
-        source = chip - 1 + 2 * t
-        return (source >= 0) & (source < chips)
-
-    def direction(turn, carry):
-        t = lax.rem(second_half + turn, 2)
-        factor_of = jnp.where(t == 0, through[0], through[1])
-
-        def piece(k, carry):
-            @pl.when(receives(t))
+    def chain(h, peer):
+        return remote(cout.at[piece(h)], cin.at[piece(h)], c_send.at[h], c_recv.at[h], ax=peer)
+
+    def back(h):
+        return remote(x2s.at[piece(h)], x2r.at[piece(h)], b_send.at[h], b_recv.at[h], ax=partner)
+
+    def advance(t, carry):
+        @pl.when(t < HARM)
+        def _():
+            eliminate(t, 0)
+            swap(t).start()
+
+        @pl.when(t == 0)
+        def _():
+            send_ends.wait_recv()
+
+        h = t - far
+
+        @pl.when((h >= 0) & (h < HARM))
+        def _():
+            swap(h).wait_recv()
+
+            @pl.when(gets)
             def _():
-                chain_copy(t, k, ax - 2 + 4 * t).wait_recv()
-
-            @pl.when(sends(t))
+                chain(h, chain_from).wait_recv()
+
+            own_factor = ends[core]
+            other_factor = part_ends[core]
+            through = own_factor * other_factor
+            for v in range(VARS):
+                c = h * VARS + v
+                x, own = cin[c], x1s[core, c]
+                cout[c] = through * x + (other_factor * own + x1r[c])
+                x2s[c] = own_factor * x + own
+
+            @pl.when(passes)
             def _():
-                for m in range(PIECE):
-                    at = k * PIECE + m
-                    cout[t, at] = factor_of * cin[t, at] + bch[t, at]
-                chain_copy(t, k, ax + 2 - 4 * t).start()
-
-            return carry
-
-        lax.fori_loop(0, CHUNKS, piece, 0)
-        return carry
-
-    lax.fori_loop(0, 2, direction, 0)
-
-    for k in range(HALF):
-        p, r = cin[0, k], cin[1, k]
-        b0, b1 = pair_values(0, k)
-        g0, g1 = pair_values(1, k)
-        p1 = alpha0 * p + b0
-        r0 = gamma1 * r + g1
-        pp[0, mine + k] = jnp.where(lower, p, p1)
-        pp[1, mine + k] = jnp.where(lower, r0, r)
-        x2s[0, k] = jnp.where(lower, p1, p)
-        x2s[1, k] = jnp.where(lower, r, r0)
-    back = remote(
-        x2s, pp.at[:, pl.ds(mine, HALF)], x_send.at[1], x_recv.at[1], ax=partner
-    )
-    back.start()
-    back_in = remote(
-        x2s, pp.at[:, pl.ds(theirs, HALF)], x_send.at[1], x_recv.at[1], ax=partner
-    )
-    back_in.wait_recv()
+                chain(h, chain_to).start()
+
+            back(h).start()
+
+        return carry
+
+    lax.fori_loop(0, HARM + chips - 1, advance, 0)
 
     def finish_copy(h):
         part = pl.ds(h * VARS, VARS)
         return pltpu.make_async_copy(bb.at[:, part], out_hbm.at[:, part], out_sem.at[h])
 
     def finish(h, carry):
+        back(h).wait_recv()
         entering, after = [], []
         for v in range(VARS):
             c = h * VARS + v
-            p = pp[0, c]
+            held, given = cin[c], x2r[c]
+            p = jnp.where(lower, held, given)
+            r = jnp.where(lower, given, held)
             whole = ends[0] * p + x1s[0, c]
             entering.append(p)
-            after.append((pp[1, c] + ends[2] * whole) / ends[3])
+            after.append((r + ends[2] * whole) * ends[3])
 
         def back_row(t, after):
             i = ROWS - 1 - t
@@ -610,10 +595,8 @@
     pitch_next.wait_send()
     pitch_prev.wait_send()
     send_ends.wait_send()
-    swap.wait_send()
-    back.wait_send()
-
-    def sent_radial(h, carry):
+
+    def sent_pieces(h, carry):
         @pl.when(rad < nrad - 1)
         def _():
             radial_up(h, rad + 1).wait_send()
@@ -622,19 +605,15 @@
         def _():
             radial_down(h, rad - 1).wait_send()
 
-        return carry
-
-    lax.fori_loop(0, HARM, sent_radial, 0)
-
-    for t in range(2):
-
-        @pl.when(sends(t))
-        def _():
-            def sent_piece(k, carry):
-                chain_copy(t, k, ax + 2 - 4 * t).wait_send()
-                return carry
-
-            lax.fori_loop(0, CHUNKS, sent_piece, 0)
+        @pl.when(passes)
+        def _():
+            chain(h, chain_to).wait_send()
+
+        swap(h).wait_send()
+        back(h).wait_send()
+        return carry
+
+    lax.fori_loop(0, HARM, sent_pieces, 0)
 
     def written(h, carry):
         finish_copy(h).wait()
@@ -671,13 +650,16 @@
             functools.partial(kernel, sizes),
             out_shape=jax.ShapeDtypeStruct((ROWS, HV) + TILE, F32),
             in_specs=[
-                pl.BlockSpec(memory_space=pl.ANY),
-                pl.BlockSpec(memory_space=pltpu.SMEM),
-                pl.BlockSpec(memory_space=pltpu.VMEM),
-                pl.BlockSpec(memory_space=pltpu.VMEM),
+                pl.BlockSpec(memory_space=pltpu.HBM),
+                pl.BlockSpec(memory_space=pltpu.HBM),
+                pl.BlockSpec(memory_space=pltpu.HBM),
+                pl.BlockSpec(memory_space=pltpu.HBM),
             ],
             out_specs=pl.BlockSpec(memory_space=pl.ANY),
             scratch_shapes=[
+                pltpu.SMEM((3, VARS, VARS), F32),
+                vmem(),
+                pltpu.VMEM((ROWS,) + TILE, jnp.int32),
                 vmem(ROWS + 2, HV),
                 vmem(ROWS, HV),
                 vmem(2, HARM, 4, VARS),
@@ -685,8 +667,8 @@
                 vmem(ROWS),
                 vmem(2, ROWS),
                 vmem(ROWS),
-                vmem(3),
-                vmem(nax, 3),
+                vmem(4),
+                vmem(nax, 4),
                 vmem(3 * VARS * VARS),
                 vmem(ROWS),
                 vmem(ROWS),
@@ -697,14 +679,13 @@
                 vmem(2, 4),
                 vmem(4),
                 vmem(2),
-                vmem(2, 2 * HALF),
-                vmem(2, HALF),
-                vmem(2, HALF),
-                vmem(2, HALF),
-                vmem(2, HALF),
-                vmem(2, HALF),
-                vmem(2, 2 * HALF),
-                dma,
+                vmem(2, HV),
+                vmem(HV),
+                vmem(HV),
+                vmem(HV),
+                vmem(HV),
+                vmem(HV),
+                dma((4,)),
                 dma((HARM,)),
                 dma((2,)),
                 dma((2,)),
@@ -716,15 +697,17 @@
                 dma((nax,)),
                 dma,
                 dma,
-                dma((2,)),
-                dma((2,)),
-                dma((2, CHUNKS)),
-                dma((2, CHUNKS)),
+                dma((HARM,)),
+                dma((HARM,)),
+                dma((HARM,)),
+                dma((HARM,)),
+                dma((HARM,)),
+                dma((HARM,)),
             ],
             compiler_params=pltpu.CompilerParams(
                 collective_id=0, has_side_effects=True, vmem_limit_bytes=40 * 1024 * 1024
             ),
-        )(to_tiles(state), flux_jac, to_tiles(line_coef), to_tiles(line_mask))
+        )(*(pltpu.with_memory_space_constraint(x, pltpu.HBM) for x in (to_tiles(state), flux_jac, to_tiles(line_coef), to_tiles(line_mask))))
         return from_tiles(out)
 
     return jax.shard_map(

time: 61.2 us -> 55.4 us (0.905)
  local copies, waits for them, and re-layouts: 5.83 us -> 1.69 us
  Pallas kernels: 55.2 us -> 53.7 us
    unnamed x9 -> x1, local copies, waits for them, and re-layouts: 5.83 us -> 1.69 us
    pallas_call x1, Pallas kernels: 55.2 us -> 53.7 us  [on_device(): pl.pallas_call(functools.partial(kernel, sizes), out_shape=jax.ShapeDtype...]
where the time goes in v2:
time: 55.4 us; the launch traced here: 55.3 us
  Pallas kernels  53.7 us (97%)
  local copies, waits for them, and re-layouts  1.69 us (3%)
    pallas_call x1, Pallas kernels, on_device(): pl.pallas_call(functools.partial(kernel, sizes), out_shape=jax.ShapeDtype...  53.7 us
    unnamed x1, local copies, waits for them, and re-layouts  1.69 us

profile of v2, /device:TPU:1, one launch (start us, length us, event | category | flops | bytes accessed | tf_op | source)
XLA Modules:
  0.0 55.3 jit_solution(11205538186346406712)
XLA Ops:
  0.0 53.7 %shard_map.46 = f32[16,49,8,128]{3,2,1,0:T(8,128)S(1)} custom-call(f32[16,49,8,128]{3,2,1,0:T(8,128)} %bitcast.21, f32[3,7,7]{2,1,0:T(8,128)} %jac_hbm.1, f32[8,128]{1,0:T(8,128)} %bitcast.23, s32[16,8,128]{2,1,0:T(8,128)} %bitcast.22), custom_call_target="tpu_custom_call" | custom-call | tf_op jit(solution)/shard_map/pallas_call | solution.py:649
  53.7 1.7 %copy.10 = f32[16,49,4,256]{3,2,1,0:T(4,128)} copy(f32[16,49,4,256]{3,2,1,0:T(4,128)S(1)} %bitcast.20) | data formatting | bytes 6422528

commit v3 on v2

--- a/solution.py
+++ b/solution.py
@@ -56,7 +56,6 @@
     dlt,
     qq,
     ww,
-    zz,
     fac,
     spd,
     spk,
@@ -68,6 +67,11 @@
     cout,
     x2s,
     x2r,
+    wl,
+    wsend,
+    wrecv,
+    part_s,
+    part_r,
     in_sem,
     out_sem,
     a_send,
@@ -86,6 +90,10 @@
     b_recv,
     c_send,
     c_recv,
+    w_send,
+    w_recv,
+    q_send,
+    q_recv,
 ):
     nax, nrad, npit = sizes
     chips = nax // 2
@@ -152,14 +160,30 @@
         return base * (1.0 + mask[i].astype(F32))
 
     a, b, c, d_, c_prev, d_prev = one, zero, zero, one, zero, one
+    heads = []
     for i in range(ROWS):
         inv = 1.0 / coef_of(i)
         dlt[i] = inv
+        heads.append(c + d_)
         c_prev, d_prev = c, d_
         a = a + inv * c
         b = b + inv * d_
         c = a + c
         d_ = b + d_
+    inv = 1.0 / (c + d_)
+    for i in range(ROWS):
+        wl[0, i] = heads[i] * inv
+    e_own = (a + b) * inv
+    n, m = one, one
+    heads = []
+    for i in reversed(range(ROWS)):
+        heads.append((i, m))
+        n = n + dlt[i] * m
+        m = n + m
+    inv = 1.0 / m
+    for i, value in heads:
+        wl[1, i] = value * inv
+    f_own = n * inv
     fs[0] = a
     fs[1] = b
     fs[2] = c_prev
@@ -173,6 +197,7 @@
                 for g in range(4):
                     for v in range(VARS):
                         rr[side, h, g, v] = zero
+                    part_r[side, h, g] = zero
                 return carry
 
             lax.fori_loop(0, HARM, clear, 0)
@@ -231,8 +256,7 @@
     row = lax.rem(sub, 4)
     is_row = [row == j for j in range(4)]
 
-    def packed(g, c):
-        rows = [st[1 + 4 * g + j, c] for j in range(4)]
+    def packed_rows(rows):
         up = rows[3]
         down = rows[0]
         for j in range(3):
@@ -240,6 +264,9 @@
         for j in range(1, 4):
             down = jnp.where(is_row[j], roll(rows[j], j, 0), down)
         return up, down
+
+    def packed(g, c):
+        return packed_rows([st[1 + 4 * g + j, c] for j in range(4)])
 
     def speed_of(x):
         return 1.0 + 0.5 * jnp.tanh(x)
@@ -297,6 +324,18 @@
 
     lax.fori_loop(0, ROWS, tables, 0)
 
+    for t in range(2):
+        for g in range(4):
+            up, down = packed_rows([fac[4 * g + j] * wl[t, 4 * g + j] for j in range(4)])
+            wsend[0, t, g] = down
+            wsend[1, t, g] = up
+
+    def weights(side, peer):
+        return remote(wsend.at[side], wrecv.at[side], w_send.at[side], w_recv.at[side], rad=peer)
+
+    def partial(side, peer):
+        return remote(part_s.at[side], part_r.at[side], q_send.at[side], q_recv.at[side], rad=peer)
+
     radial_peers = jnp.minimum(rad, 1) + jnp.minimum(nrad - 1 - rad, 1)
     pl.semaphore_wait(barrier, nax - 1 + 2 + radial_peers)
     pitch_next.start()
@@ -321,7 +360,15 @@
 
         return carry
 
-    lax.fori_loop(0, HARM, send_radial, 0)
+    @pl.when(rad > 0)
+    def _():
+        weights(0, rad - 1).start()
+
+    @pl.when(rad < nrad - 1)
+    def _():
+        weights(1, rad + 1).start()
+
+    lax.fori_loop(0, 2, send_radial, 0)
 
     def send_factor(step, carry):
         factor(step).start()
@@ -329,6 +376,41 @@
 
     lax.fori_loop(1, nax, send_factor, 0)
 
+
+    def weigh(side):
+        def harmonic(h, carry):
+            for pair_at in range(4):
+                got = zero
+                for m in range(4):
+                    v = 2 * pair_at + m // 2
+                    if v == VARS:
+                        continue
+                    x = zero
+                    for g in range(4):
+                        x = x + wrecv[side, m % 2, g] * rs[side, h, g, v]
+                    turn = 1 if side else -1
+                    x = x + roll(x, turn, 0)
+                    x = x + roll(x, 2 * turn, 0)
+                    target = 3 - m if side else m
+                    got = jnp.where(is_row[target], roll(x, -turn * m, 0), got)
+                part_s[side, h, pair_at] = got
+            return carry
+
+        lax.fori_loop(0, HARM, harmonic, 0)
+
+    @pl.when(rad < nrad - 1)
+    def _():
+        weights(0, rad + 1).wait_recv()
+        weigh(0)
+        partial(0, rad + 1).start()
+
+    @pl.when(rad > 0)
+    def _():
+        weights(1, rad - 1).wait_recv()
+        weigh(1)
+        partial(1, rad - 1).start()
+
+    lax.fori_loop(2, HARM, send_radial, 0)
 
     pitch_next.wait_recv()
     pitch_prev.wait_recv()
@@ -442,14 +524,10 @@
         m = after
     e_out = n * inv
     n, m = f_in, one
-    values = []
     for i in reversed(range(ROWS)):
-        values.append((i, m))
         n = n + dlt[i] * m
         m = n + m
     inv = 1.0 / m
-    for i, value in values:
-        zz[i] = value * inv
     ends[0] = ww[ROWS - 1]
     ends[1] = inv
     ends[2] = 1.0 - f_in
@@ -459,6 +537,53 @@
 
     edge_low = is_row[0]
     edge_high = is_row[3]
+    lower = core == 0
+
+    def piece(h):
+        return pl.ds(h * VARS, VARS)
+
+    def swap(h):
+        return remote(
+            x1s.at[1 - core, piece(h)], x1r.at[piece(h)], s_send.at[h], s_recv.at[h], ax=partner
+        )
+
+    @pl.when(rad > 0)
+    def _():
+        partial(0, rad - 1).wait_recv()
+
+    @pl.when(rad < nrad - 1)
+    def _():
+        partial(1, rad + 1).wait_recv()
+
+    q_in, s_in = 1.0 - e_in, 1.0 - f_in
+    mix_first = wl[1, ROWS - 1] * q_in / (e_in + f_own * q_in)
+    mix_last = wl[0, 0] * s_in / (f_in + e_own * s_in)
+
+    def block_ends(h, carry):
+        def group(g, sums):
+            sums = list(sums)
+            for j in range(4):
+                i = 4 * g + j
+                last, first = wl[0, i], wl[1, i]
+                for v in range(VARS):
+                    right = bb[i, h * VARS + v]
+                    sums[2 * v] = sums[2 * v] + last * right
+                    sums[2 * v + 1] = sums[2 * v + 1] + first * right
+            return tuple(sums)
+
+        sums = list(lax.fori_loop(0, 4, group, (zero,) * (2 * VARS)))
+        for at in range(2 * VARS):
+            m = at % 4
+            low = roll(part_r[0, h, at // 4], -m, 0)
+            high = roll(part_r[1, h, at // 4], m, 0)
+            sums[at] = sums[at] + jnp.where(edge_low, low, jnp.where(edge_high, high, 0.0))
+        for v in range(VARS):
+            x1s[0, h * VARS + v] = sums[2 * v] + mix_first * sums[2 * v + 1]
+            x1s[1, h * VARS + v] = sums[2 * v + 1] + mix_last * sums[2 * v]
+        swap(h).start()
+        return carry
+
+    lax.fori_loop(0, HARM, block_ends, 0)
 
     def eliminate(h, carry):
         @pl.when(rad > 0)
@@ -470,36 +595,21 @@
             radial_down(h, rad + 1).wait_recv()
 
         def group(g, carry):
-            carried, sums = list(carry[0]), list(carry[1])
+            carried = list(carry)
             for j in range(4):
                 i = 4 * g + j
-                scale, q, z = fac[i], qq[i], zz[i]
+                scale, q = fac[i], qq[i]
                 for v in range(VARS):
                     low = roll(rr[0, h, g, v], -j, 0)
                     high = roll(rr[1, h, g, v], 3 - j, 0)
                     extra = jnp.where(edge_low, low, jnp.where(edge_high, high, 0.0))
                     right = bb[i, h * VARS + v] + scale * extra
                     carried[v] = q * (right + carried[v])
-                    sums[v] = sums[v] + z * right
                     bb[i, h * VARS + v] = carried[v]
-            return tuple(carried), tuple(sums)
-
-        zeros = (zero,) * VARS
-        carried, sums = lax.fori_loop(0, 4, group, (zeros, zeros))
-        for v in range(VARS):
-            x1s[0, h * VARS + v] = carried[v]
-            x1s[1, h * VARS + v] = sums[v]
-        return carry
-
-    lower = core == 0
-
-    def piece(h):
-        return pl.ds(h * VARS, VARS)
-
-    def swap(h):
-        return remote(
-            x1s.at[1 - core, piece(h)], x1r.at[piece(h)], s_send.at[h], s_recv.at[h], ax=partner
-        )
+            return tuple(carried)
+
+        lax.fori_loop(0, 4, group, (zero,) * VARS)
+        return carry
 
     def chain(h, peer):
         return remote(cout.at[piece(h)], cin.at[piece(h)], c_send.at[h], c_recv.at[h], ax=peer)
@@ -507,44 +617,45 @@
     def back(h):
         return remote(x2s.at[piece(h)], x2r.at[piece(h)], b_send.at[h], b_recv.at[h], ax=partner)
 
-    def advance(t, carry):
-        @pl.when(t < HARM)
-        def _():
-            eliminate(t, 0)
-            swap(t).start()
+    send_ends.wait_recv()
+
+    def relay(h, carry):
+        swap(h).wait_recv()
+
+        @pl.when(gets)
+        def _():
+            chain(h, chain_from).wait_recv()
+
+        own_factor = ends[core]
+        other_factor = part_ends[core]
+        through = own_factor * other_factor
+        for v in range(VARS):
+            c = h * VARS + v
+            x, own = cin[c], x1s[core, c]
+            cout[c] = through * x + (other_factor * own + x1r[c])
+            x2s[c] = own_factor * x + own
+
+        @pl.when(passes)
+        def _():
+            chain(h, chain_to).start()
+
+        back(h).start()
+        return carry
+
+    relay_turn = lax.div(far, 5)
+
+    def turn(t, carry):
+        @pl.when(t == relay_turn)
+        def _():
+            lax.fori_loop(0, HARM, relay, 0)
 
         @pl.when(t == 0)
         def _():
-            send_ends.wait_recv()
-
-        h = t - far
-
-        @pl.when((h >= 0) & (h < HARM))
-        def _():
-            swap(h).wait_recv()
-
-            @pl.when(gets)
-            def _():
-                chain(h, chain_from).wait_recv()
-
-            own_factor = ends[core]
-            other_factor = part_ends[core]
-            through = own_factor * other_factor
-            for v in range(VARS):
-                c = h * VARS + v
-                x, own = cin[c], x1s[core, c]
-                cout[c] = through * x + (other_factor * own + x1r[c])
-                x2s[c] = own_factor * x + own
-
-            @pl.when(passes)
-            def _():
-                chain(h, chain_to).start()
-
-            back(h).start()
-
-        return carry
-
-    lax.fori_loop(0, HARM + chips - 1, advance, 0)
+            lax.fori_loop(0, HARM, eliminate, 0)
+
+        return carry
+
+    lax.fori_loop(0, 2, turn, 0)
 
     def finish_copy(h):
         part = pl.ds(h * VARS, VARS)
@@ -595,6 +706,16 @@
     pitch_next.wait_send()
     pitch_prev.wait_send()
     send_ends.wait_send()
+
+    @pl.when(rad > 0)
+    def _():
+        weights(0, rad - 1).wait_send()
+        partial(1, rad - 1).wait_send()
+
+    @pl.when(rad < nrad - 1)
+    def _():
+        weights(1, rad + 1).wait_send()
+        partial(0, rad + 1).wait_send()
 
     def sent_pieces(h, carry):
         @pl.when(rad < nrad - 1)
@@ -674,7 +795,6 @@
                 vmem(ROWS),
                 vmem(ROWS),
                 vmem(ROWS),
-                vmem(ROWS),
                 vmem(ROWS + 2),
                 vmem(2, 4),
                 vmem(4),
@@ -685,6 +805,11 @@
                 vmem(HV),
                 vmem(HV),
                 vmem(HV),
+                vmem(2, ROWS),
+                vmem(2, 2, 4),
+                vmem(2, 2, 4),
+                vmem(2, HARM, 4),
+                vmem(2, HARM, 4),
                 dma((4,)),
                 dma((HARM,)),
                 dma((2,)),
@@ -703,6 +828,10 @@
                 dma((HARM,)),
                 dma((HARM,)),
                 dma((HARM,)),
+                dma((2,)),
+                dma((2,)),
+                dma((2,)),
+                dma((2,)),
             ],
             compiler_params=pltpu.CompilerParams(
                 collective_id=0, has_side_effects=True, vmem_limit_bytes=40 * 1024 * 1024

time: 55.4 us -> 49.4 us (0.89)
  Pallas kernels: 53.7 us -> 47.7 us
    pallas_call x1, Pallas kernels: 53.7 us -> 47.7 us  [on_device(): pl.pallas_call(functools.partial(kernel, sizes), out_shape=jax.ShapeDtype...]
where the time goes in v3:
time: 49.4 us
  Pallas kernels  47.7 us (97%)
  local copies, waits for them, and re-layouts  1.69 us (3%)
    pallas_call x1, Pallas kernels, on_device(): pl.pallas_call(functools.partial(kernel, sizes), out_shape=jax.ShapeDtype...  47.7 us
    unnamed x1, local copies, waits for them, and re-layouts  1.69 us

profile of v3, /device:TPU:1, one launch (start us, length us, event | category | flops | bytes accessed | tf_op | source)
XLA Modules:
  0.0 49.4 jit_solution(16465667903643410872)
XLA Ops:
  0.0 47.7 %shard_map.46 = f32[16,49,8,128]{3,2,1,0:T(8,128)S(1)} custom-call(f32[16,49,8,128]{3,2,1,0:T(8,128)} %bitcast.21, f32[3,7,7]{2,1,0:T(8,128)} %jac_hbm.1, f32[8,128]{1,0:T(8,128)} %bitcast.23, s32[16,8,128]{2,1,0:T(8,128)} %bitcast.22), custom_call_target="tpu_custom_call" | custom-call | tf_op jit(solution)/shard_map/pallas_call | solution.py:770
  47.7 1.7 %copy.10 = f32[16,49,4,256]{3,2,1,0:T(4,128)} copy(f32[16,49,4,256]{3,2,1,0:T(4,128)S(1)} %bitcast.20) | data formatting | bytes 6422528

commit v4 on v3

--- a/solution.py
+++ b/solution.py
@@ -51,7 +51,9 @@
     pr,
     pe,
     fs,
-    fr,
+    fx,
+    mo,
+    mi,
     am,
     dlt,
     qq,
@@ -80,8 +82,8 @@
     r_recv,
     p_send,
     p_recv,
-    f_send,
-    f_recv,
+    g_send,
+    g_recv,
     e_send,
     e_recv,
     s_send,
@@ -119,13 +121,14 @@
 
     barrier = pltpu.get_barrier_semaphore()
 
-    def greet(step, carry):
-        pl.semaphore_signal(
-            barrier, inc=1, device_id={"ax": lax.rem(ax + step, nax)}, device_id_type=MESH
-        )
-        return carry
-
-    lax.fori_loop(1, nax, greet, 0)
+    for offset in (-2, -1, 1, 2):
+
+        @pl.when((ax + offset >= 0) & (ax + offset < nax))
+        def _():
+            pl.semaphore_signal(
+                barrier, inc=1, device_id={"ax": ax + offset}, device_id_type=MESH
+            )
+
     pl.semaphore_signal(barrier, inc=1, device_id={"pit": pit_next}, device_id_type=MESH)
     pl.semaphore_signal(barrier, inc=1, device_id={"pit": pit_prev}, device_id_type=MESH)
 
@@ -226,6 +229,7 @@
 
     @pl.when(far == 0)
     def _():
+        mi[1] = one
         for c in range(HV):
             cin[c] = zero
 
@@ -243,10 +247,11 @@
     pair = lax.div(lane, 2)
 
     def pack(i, carry):
-        got = zero
+        got = [zero] * 4
         for c in range(HV):
-            got = jnp.where(pair == c, roll(st[1 + i, c], 2 * c + 1, 1), got)
-        ps[i] = got
+            k = c * 4 // HV
+            got[k] = jnp.where(pair == c, roll(st[1 + i, c], 2 * c + 1, 1), got[k])
+        ps[i] = (got[0] + got[1]) + (got[2] + got[3])
         return carry
 
     lax.fori_loop(0, ROWS, pack, 0)
@@ -271,16 +276,102 @@
     def speed_of(x):
         return 1.0 + 0.5 * jnp.tanh(x)
 
+    def tables(i, carry):
+        s = speed_of(st[1 + i, 0])
+        spd[1 + i] = s
+        coef = coef_of(i)
+        radius = s * limit + (6.0 * dissipation + HARM // 2 * blade_freq)
+        fac[i] = (-0.5 * section_weight * courant) * jnp.sqrt(1.0 + 4.0 * coef) / (coef * radius)
+        return carry
+
+    lax.fori_loop(0, ROWS, tables, 0)
+
+    for t in range(2):
+        for g in range(4):
+            up, down = packed_rows([fac[4 * g + j] * wl[t, 4 * g + j] for j in range(4)])
+            wsend[0, t, g] = down
+            wsend[1, t, g] = up
+
+    def weights(side, peer):
+        return remote(wsend.at[side], wrecv.at[side], w_send.at[side], w_recv.at[side], rad=peer)
+
+    swap_blocks = remote(fs, fx, g_send.at[0], g_recv.at[0], ax=partner)
+    tell = remote(mo.at[0], mi.at[0], g_send.at[1], g_recv.at[1], ax=partner)
+
+    def pass_pivot(peer):
+        return remote(mo.at[1], mi.at[1], g_send.at[2], g_recv.at[2], ax=peer)
+
+    lower = core == 0
+
+    def through_block(block, x):
+        a, b, c_prev, d_prev = (block[k] for k in range(4))
+        low = jnp.where(lower, a + c_prev, c_prev + d_prev)
+        high = jnp.where(lower, b + d_prev, a + b)
+        return (jnp.where(lower, a, d_prev) * x + b) / (low * x + high)
+
+    def serve_pivots():
+        swap_blocks.wait_recv()
+
+        @pl.when(gets)
+        def _():
+            pass_pivot(chain_from).wait_recv()
+
+        inner = through_block(fs, mi[1])
+        mo[0] = inner
+        mo[1] = through_block(fx, inner)
+        tell.start()
+
+        @pl.when(passes)
+        def _():
+            pass_pivot(chain_to).start()
+
+    def partial(side, peer):
+        return remote(part_s.at[side], part_r.at[side], q_send.at[side], q_recv.at[side], rad=peer)
+
+    radial_peers = jnp.minimum(rad, 1) + jnp.minimum(nrad - 1 - rad, 1)
+    axial_peers = jnp.minimum(ax, 2) + jnp.minimum(nax - 1 - ax, 2)
+    pl.semaphore_wait(barrier, 2 + axial_peers + radial_peers)
+    swap_blocks.start()
+    pitch_next.start()
+    pitch_prev.start()
+
+    @pl.when(ax < nax - 1)
+    def _():
+        axial_up(ax + 1).start()
+
+    @pl.when(ax > 0)
+    def _():
+        axial_down(ax - 1).start()
+
+    @pl.when(rad > 0)
+    def _():
+        weights(0, rad - 1).start()
+
+    @pl.when(rad < nrad - 1)
+    def _():
+        weights(1, rad + 1).start()
+
+    def radial_up(h, peer):
+        return remote(rs.at[0, h], rr.at[0, h], r_send.at[0, h], r_recv.at[0, h], rad=peer)
+
+    def radial_down(h, peer):
+        return remote(rs.at[1, h], rr.at[1, h], r_send.at[1, h], r_recv.at[1, h], rad=peer)
+
+    def send_radial(h, carry):
+        @pl.when(rad < nrad - 1)
+        def _():
+            radial_up(h, rad + 1).start()
+
+        @pl.when(rad > 0)
+        def _():
+            radial_down(h, rad - 1).start()
+
+        return carry
+
     for g in range(4):
         up, down = packed(g, 0)
         spk[0, g] = speed_of(up)
         spk[1, g] = speed_of(down)
-
-    def radial_up(h, peer):
-        return remote(rs.at[0, h], rr.at[0, h], r_send.at[0, h], r_recv.at[0, h], rad=peer)
-
-    def radial_down(h, peer):
-        return remote(rs.at[1, h], rr.at[1, h], r_send.at[1, h], r_recv.at[1, h], rad=peer)
 
     def radial(h, carry):
         def group(g, carry):
@@ -305,77 +396,17 @@
 
         lax.fori_loop(0, 4, group, 0)
 
+        @pl.when(h < 2)
+        def _():
+            send_radial(h, 0)
+
         return carry
 
     lax.fori_loop(0, HARM, radial, 0)
 
-    def factor(step):
-        return remote(
-            fs, fr.at[ax], f_send.at[step], f_recv.at[ax], ax=lax.rem(ax + step, nax)
-        )
-
-    def tables(i, carry):
-        s = speed_of(st[1 + i, 0])
-        spd[1 + i] = s
-        coef = coef_of(i)
-        radius = s * limit + (6.0 * dissipation + HARM // 2 * blade_freq)
-        fac[i] = (-0.5 * section_weight * courant) * jnp.sqrt(1.0 + 4.0 * coef) / (coef * radius)
-        return carry
-
-    lax.fori_loop(0, ROWS, tables, 0)
-
-    for t in range(2):
-        for g in range(4):
-            up, down = packed_rows([fac[4 * g + j] * wl[t, 4 * g + j] for j in range(4)])
-            wsend[0, t, g] = down
-            wsend[1, t, g] = up
-
-    def weights(side, peer):
-        return remote(wsend.at[side], wrecv.at[side], w_send.at[side], w_recv.at[side], rad=peer)
-
-    def partial(side, peer):
-        return remote(part_s.at[side], part_r.at[side], q_send.at[side], q_recv.at[side], rad=peer)
-
-    radial_peers = jnp.minimum(rad, 1) + jnp.minimum(nrad - 1 - rad, 1)
-    pl.semaphore_wait(barrier, nax - 1 + 2 + radial_peers)
-    pitch_next.start()
-    pitch_prev.start()
-
-    @pl.when(ax < nax - 1)
-    def _():
-        axial_up(ax + 1).start()
-
-    @pl.when(ax > 0)
-    def _():
-        axial_down(ax - 1).start()
-
-    def send_radial(h, carry):
-        @pl.when(rad < nrad - 1)
-        def _():
-            radial_up(h, rad + 1).start()
-
-        @pl.when(rad > 0)
-        def _():
-            radial_down(h, rad - 1).start()
-
-        return carry
-
-    @pl.when(rad > 0)
-    def _():
-        weights(0, rad - 1).start()
-
-    @pl.when(rad < nrad - 1)
-    def _():
-        weights(1, rad + 1).start()
-
-    lax.fori_loop(0, 2, send_radial, 0)
-
-    def send_factor(step, carry):
-        factor(step).start()
-        return carry
-
-    lax.fori_loop(1, nax, send_factor, 0)
-
+    @pl.when(far < 5)
+    def _():
+        serve_pivots()
 
     def weigh(side):
         def harmonic(h, carry):
@@ -398,79 +429,40 @@
 
         lax.fori_loop(0, HARM, harmonic, 0)
 
-    @pl.when(rad < nrad - 1)
-    def _():
-        weights(0, rad + 1).wait_recv()
-        weigh(0)
-        partial(0, rad + 1).start()
-
-    @pl.when(rad > 0)
-    def _():
-        weights(1, rad - 1).wait_recv()
-        weigh(1)
-        partial(1, rad - 1).start()
-
-    lax.fori_loop(2, HARM, send_radial, 0)
-
-    pitch_next.wait_recv()
-    pitch_prev.wait_recv()
-    top = sub >= 4
-    even = lax.rem(lane, 2) == 0
-
-    def merge(i, carry):
-        own = ps[i]
-        before = jnp.where(top, pr[0, i], own)
-        after = jnp.where(top, own, pr[1, i])
-        both = jnp.where(even, roll(after, -1, 1), roll(before, 1, 1))
-        pe[i] = roll(both, 4, 0)
-        return carry
-
-    lax.fori_loop(0, ROWS, merge, 0)
+    def return_sums():
+        @pl.when(rad < nrad - 1)
+        def _():
+            weights(0, rad + 1).wait_recv()
+            weigh(0)
+            partial(0, rad + 1).start()
+
+        @pl.when(rad > 0)
+        def _():
+            weights(1, rad - 1).wait_recv()
+            weigh(1)
+            partial(1, rad - 1).start()
+
+        lax.fori_loop(2, HARM, send_radial, 0)
 
     first_lane = lane == 0
     last_lane = lane == 127
     inner_low = row > 0
     inner_high = row < 3
 
-    def sides(step, carry):
-        @pl.when(step == ROWS - 2)
-        def _():
-            @pl.when(ax > 0)
-            def _():
-                axial_up(ax - 1).wait_recv()
-
-            @pl.when(ax < nax - 1)
-            def _():
-                axial_down(ax + 1).wait_recv()
-
-            spd[0] = speed_of(st[0, 0])
-            spd[ROWS + 1] = speed_of(st[ROWS + 1, 0])
-
-        i = lax.rem(step + 1, ROWS)
-        pitched = pe[i]
+    def straight(i):
         sa, sc, sb = spd[i], spd[1 + i], spd[2 + i]
         su = roll(sc, 1, 0)
         sd = roll(sc, -1, 0)
-        scale = fac[i]
-        sl = sr = None
-        middle = []
-        accs = []
         for h in range(HARM):
-            d0, d1, d2, acc = [], [], [], []
+            d0, d1, acc = [], [], []
             for v in range(VARS):
                 c = h * VARS + v
                 here, back, ahead = st[1 + i, c], st[i, c], st[2 + i, c]
-                e = roll(pitched, -(2 * c + 1), 1)
-                left = jnp.where(first_lane, e, roll(here, 1, 1))
-                right = jnp.where(last_lane, e, roll(here, -1, 1))
-                if c == 0:
-                    sl, sr = speed_of(left), speed_of(right)
                 under = jnp.where(inner_low, roll(here, 1, 0), 0.0)
                 over = jnp.where(inner_high, roll(here, -1, 0), 0.0)
                 d0.append(sb * ahead - sa * back)
                 d1.append(sd * over - su * under)
-                d2.append(sr * right - sl * left)
-                around = ((back + ahead) + (left + right)) + (under + over)
+                around = (back + ahead) + (under + over)
                 acc.append(12.0 * dissipation * here - 2.0 * dissipation * around)
                 if h:
                     k = (h + 1) // 2
@@ -482,37 +474,86 @@
                 for w in range(VARS):
                     t = t + am[v * 7 + w] * d0[w]
                     t = t + am[49 + v * 7 + w] * d1[w]
+                bb[i, h * VARS + v] = t
+
+    def inner_rows(step, carry):
+        @pl.when(step == 6)
+        def _():
+            return_sums()
+
+        straight(step + 1)
+        return carry
+
+    lax.fori_loop(0, ROWS - 2, inner_rows, 0)
+
+    @pl.when(ax > 0)
+    def _():
+        axial_up(ax - 1).wait_recv()
+
+    @pl.when(ax < nax - 1)
+    def _():
+        axial_down(ax + 1).wait_recv()
+
+    spd[0] = speed_of(st[0, 0])
+    spd[ROWS + 1] = speed_of(st[ROWS + 1, 0])
+
+    def outer_rows(step, carry):
+        straight((ROWS - 1) * step)
+        return carry
+
+    lax.fori_loop(0, 2, outer_rows, 0)
+
+    @pl.when(far == 5)
+    def _():
+        serve_pivots()
+
+    pitch_next.wait_recv()
+    pitch_prev.wait_recv()
+    top = sub >= 4
+    even = lax.rem(lane, 2) == 0
+
+    def merge(i, carry):
+        own = ps[i]
+        before = jnp.where(top, pr[0, i], own)
+        after = jnp.where(top, own, pr[1, i])
+        both = jnp.where(even, roll(after, -1, 1), roll(before, 1, 1))
+        pe[i] = roll(both, 4, 0)
+        return carry
+
+    lax.fori_loop(0, ROWS, merge, 0)
+
+    def sideways(i, carry):
+        pitched = pe[i]
+        scale = fac[i]
+        sl = sr = None
+        for h in range(HARM):
+            d2, acc = [], []
+            for v in range(VARS):
+                c = h * VARS + v
+                here = st[1 + i, c]
+                e = roll(pitched, -(2 * c + 1), 1)
+                left = jnp.where(first_lane, e, roll(here, 1, 1))
+                right = jnp.where(last_lane, e, roll(here, -1, 1))
+                if c == 0:
+                    sl, sr = speed_of(left), speed_of(right)
+                d2.append(sr * right - sl * left)
+                acc.append(bb[i, c] - 2.0 * dissipation * (left + right))
+            for v in range(VARS):
+                t = acc[v]
+                for w in range(VARS):
                     t = t + am[98 + v * 7 + w] * d2[w]
                 bb[i, h * VARS + v] = scale * t
         return carry
 
-    lax.fori_loop(0, ROWS, sides, 0)
-
-    def arrive(step, carry):
-        source = lax.rem(ax + nax - step, nax)
-        remote(fs, fr.at[source], f_send.at[step], f_recv.at[source], ax=source).wait_recv()
-        return carry
-
-    lax.fori_loop(1, nax, arrive, 0)
-
-    def entries(j):
-        return fr[j, 0], fr[j, 1], fr[j, 2], fr[j, 3]
-
-    def ahead_of(j, carry):
-        n, m = carry
-        a, b, c_prev, d_prev = entries(j)
-        return a * n + b * m, (a + c_prev) * n + (b + d_prev) * m
-
-    n, m = lax.fori_loop(0, ax, ahead_of, (one, one))
-    e_in = n / m
-
-    def behind(t, carry):
-        n, m = carry
-        a, b, c_prev, d_prev = entries(nax - 1 - t)
-        return d_prev * n + b * m, (c_prev + d_prev) * n + (a + b) * m
-
-    n, m = lax.fori_loop(0, nax - 1 - ax, behind, (one, one))
-    f_in = n / m
+    lax.fori_loop(0, ROWS, sideways, 0)
+
+    @pl.when(far > 5)
+    def _():
+        serve_pivots()
+
+    tell.wait_recv()
+    e_in = jnp.where(lower, mi[1], mi[0])
+    f_in = jnp.where(lower, mi[0], mi[1])
 
     n, m = e_in, one
     for i in range(ROWS):
@@ -537,8 +578,6 @@
 
     edge_low = is_row[0]
     edge_high = is_row[3]
-    lower = core == 0
-
     def piece(h):
         return pl.ds(h * VARS, VARS)
 
@@ -698,11 +737,13 @@
     def _():
         axial_down(ax - 1).wait_send()
 
-    def sent(step, carry):
-        factor(step).wait_send()
-        return carry
-
-    lax.fori_loop(1, nax, sent, 0)
+    swap_blocks.wait_send()
+    tell.wait_send()
+
+    @pl.when(passes)
+    def _():
+        pass_pivot(chain_to).wait_send()
+
     pitch_next.wait_send()
     pitch_prev.wait_send()
     send_ends.wait_send()
@@ -789,7 +830,9 @@
                 vmem(2, ROWS),
                 vmem(ROWS),
                 vmem(4),
-                vmem(nax, 4),
+                vmem(4),
+                vmem(2),
+                vmem(2),
                 vmem(3 * VARS * VARS),
                 vmem(ROWS),
                 vmem(ROWS),
@@ -818,8 +861,8 @@
                 dma((2, HARM)),
                 dma((2,)),
                 dma((2,)),
-                dma((nax,)),
-                dma((nax,)),
+                dma((3,)),
+                dma((3,)),
                 dma,
                 dma,
                 dma((HARM,)),

time: 49.4 us -> 50.7 us (1.026)
  Pallas kernels: 47.7 us -> 48.9 us
    pallas_call x1, Pallas kernels: 47.7 us -> 48.9 us  [on_device(): pl.pallas_call(functools.partial(kernel, sizes), out_shape=jax.ShapeDtype...]
where the time goes in v4:
time: 50.7 us; the launch traced here: 50.6 us
  Pallas kernels  48.9 us (96%)
  local copies, waits for them, and re-layouts  1.69 us (3%)
    pallas_call x1, Pallas kernels, on_device(): pl.pallas_call(functools.partial(kernel, sizes), out_shape=jax.ShapeDtype...  48.9 us
    unnamed x1, local copies, waits for them, and re-layouts  1.69 us

profile of v4, /device:TPU:1, one launch (start us, length us, event | category | flops | bytes accessed | tf_op | source)
XLA Modules:
  0.0 50.6 jit_solution(13126472480125733244)
XLA Ops:
  0.0 48.9 %shard_map.46 = f32[16,49,8,128]{3,2,1,0:T(8,128)S(1)} custom-call(f32[16,49,8,128]{3,2,1,0:T(8,128)} %bitcast.21, f32[3,7,7]{2,1,0:T(8,128)} %jac_hbm.1, f32[8,128]{1,0:T(8,128)} %bitcast.23, s32[16,8,128]{2,1,0:T(8,128)} %bitcast.22), custom_call_target="tpu_custom_call" | custom-call | tf_op jit(solution)/shard_map/pallas_call | solution.py:811
  48.9 1.7 %copy.10 = f32[16,49,4,256]{3,2,1,0:T(4,128)} copy(f32[16,49,4,256]{3,2,1,0:T(4,128)S(1)} %bitcast.20) | data formatting | bytes 6422528

commit v5 on v4

--- a/solution.py
+++ b/solution.py
@@ -11,6 +11,9 @@
 VARS = 7
 HV = HARM * VARS
 ROWS = 16
+PIECE = 3
+PIECES = -(-HV // PIECE)
+PAD = PIECE * PIECES
 MESH = pl.DeviceIdType.MESH
 
 blade_freq = 0.6
@@ -62,8 +65,9 @@
     spd,
     spk,
     ends,
-    part_ends,
+    products,
     x1s,
+    xt,
     x1r,
     cin,
     cout,
@@ -84,8 +88,6 @@
     p_recv,
     g_send,
     g_recv,
-    e_send,
-    e_recv,
     s_send,
     s_recv,
     b_send,
@@ -230,7 +232,7 @@
     @pl.when(far == 0)
     def _():
         mi[1] = one
-        for c in range(HV):
+        for c in range(PAD):
             cin[c] = zero
 
     load.wait()
@@ -307,7 +309,8 @@
         a, b, c_prev, d_prev = (block[k] for k in range(4))
         low = jnp.where(lower, a + c_prev, c_prev + d_prev)
         high = jnp.where(lower, b + d_prev, a + b)
-        return (jnp.where(lower, a, d_prev) * x + b) / (low * x + high)
+        inv = 1.0 / (low * x + high)
+        return (jnp.where(lower, a, d_prev) * x + b) * inv, inv
 
     def serve_pivots():
         swap_blocks.wait_recv()
@@ -316,9 +319,12 @@
         def _():
             pass_pivot(chain_from).wait_recv()
 
-        inner = through_block(fs, mi[1])
+        inner, own = through_block(fs, mi[1])
+        outer, other = through_block(fx, inner)
         mo[0] = inner
-        mo[1] = through_block(fx, inner)
+        mo[1] = outer
+        products[0] = own
+        products[1] = other
         tell.start()
 
         @pl.when(passes)
@@ -404,7 +410,7 @@
 
     lax.fori_loop(0, HARM, radial, 0)
 
-    @pl.when(far < 5)
+    @pl.when(far < 2)
     def _():
         serve_pivots()
 
@@ -503,7 +509,7 @@
 
     lax.fori_loop(0, 2, outer_rows, 0)
 
-    @pl.when(far == 5)
+    @pl.when((far >= 2) & (far < 4))
     def _():
         serve_pivots()
 
@@ -547,45 +553,22 @@
 
     lax.fori_loop(0, ROWS, sideways, 0)
 
-    @pl.when(far > 5)
-    def _():
-        serve_pivots()
-
-    tell.wait_recv()
-    e_in = jnp.where(lower, mi[1], mi[0])
-    f_in = jnp.where(lower, mi[0], mi[1])
-
-    n, m = e_in, one
-    for i in range(ROWS):
-        n = n + dlt[i] * m
-        after = n + m
-        inv = 1.0 / after
-        qq[i] = m * inv
-        ww[i] = inv
-        m = after
-    e_out = n * inv
-    n, m = f_in, one
-    for i in reversed(range(ROWS)):
-        n = n + dlt[i] * m
-        m = n + m
-    inv = 1.0 / m
-    ends[0] = ww[ROWS - 1]
-    ends[1] = inv
-    ends[2] = 1.0 - f_in
-    ends[3] = 1.0 / (e_out + f_in * qq[ROWS - 1])
-    send_ends = remote(ends.at[pl.ds(0, 2)], part_ends, e_send, e_recv, ax=partner)
-    send_ends.start()
-
     edge_low = is_row[0]
     edge_high = is_row[3]
-    def piece(h):
-        return pl.ds(h * VARS, VARS)
-
-    def swap(h):
+    def piece(k):
+        return pl.ds(k * PIECE, PIECE)
+
+    def swap(k):
         return remote(
-            x1s.at[1 - core, piece(h)], x1r.at[piece(h)], s_send.at[h], s_recv.at[h], ax=partner
+            xt.at[1 - core, piece(k)], x1r.at[piece(k)], s_send.at[k], s_recv.at[k], ax=partner
         )
 
+    def chain(k, peer):
+        return remote(cout.at[piece(k)], cin.at[piece(k)], c_send.at[k], c_recv.at[k], ax=peer)
+
+    def back(k):
+        return remote(x2s.at[piece(k)], x2r.at[piece(k)], b_send.at[k], b_recv.at[k], ax=partner)
+
     @pl.when(rad > 0)
     def _():
         partial(0, rad - 1).wait_recv()
@@ -593,10 +576,6 @@
     @pl.when(rad < nrad - 1)
     def _():
         partial(1, rad + 1).wait_recv()
-
-    q_in, s_in = 1.0 - e_in, 1.0 - f_in
-    mix_first = wl[1, ROWS - 1] * q_in / (e_in + f_own * q_in)
-    mix_last = wl[0, 0] * s_in / (f_in + e_own * s_in)
 
     def block_ends(h, carry):
         def group(g, sums):
@@ -617,12 +596,18 @@
             high = roll(part_r[1, h, at // 4], m, 0)
             sums[at] = sums[at] + jnp.where(edge_low, low, jnp.where(edge_high, high, 0.0))
         for v in range(VARS):
-            x1s[0, h * VARS + v] = sums[2 * v] + mix_first * sums[2 * v + 1]
-            x1s[1, h * VARS + v] = sums[2 * v + 1] + mix_last * sums[2 * v]
-        swap(h).start()
+            x1s[0, h * VARS + v] = sums[2 * v]
+            x1s[1, h * VARS + v] = sums[2 * v + 1]
         return carry
 
     lax.fori_loop(0, HARM, block_ends, 0)
+    for t in range(2):
+        for c in range(HV, PAD):
+            x1s[t, c] = zero
+
+    def share(x, edge):
+        rest = 1.0 - x
+        return wl[0, 0] * rest / (x + edge * rest)
 
     def eliminate(h, carry):
         @pl.when(rad > 0)
@@ -650,67 +635,109 @@
         lax.fori_loop(0, 4, group, (zero,) * VARS)
         return carry
 
-    def chain(h, peer):
-        return remote(cout.at[piece(h)], cin.at[piece(h)], c_send.at[h], c_recv.at[h], ax=peer)
-
-    def back(h):
-        return remote(x2s.at[piece(h)], x2r.at[piece(h)], b_send.at[h], b_recv.at[h], ax=partner)
-
-    send_ends.wait_recv()
-
-    def relay(h, carry):
-        swap(h).wait_recv()
-
-        @pl.when(gets)
-        def _():
-            chain(h, chain_from).wait_recv()
-
-        own_factor = ends[core]
-        other_factor = part_ends[core]
+    def give():
+        tell.wait_recv()
+        part = share(mi[0], jnp.where(lower, e_own, f_own))
+
+        def one_piece(k, carry):
+            for m in range(PIECE):
+                c = k * PIECE + m
+                xt[1 - core, c] = x1s[1 - core, c] + part * x1s[core, c]
+            swap(k).start()
+            return carry
+
+        lax.fori_loop(0, PIECES, one_piece, 0)
+
+    def relay_all():
+        part = share(mi[1], jnp.where(lower, f_own, e_own))
+        own_factor = products[0]
+        other_factor = products[1]
         through = own_factor * other_factor
-        for v in range(VARS):
-            c = h * VARS + v
-            x, own = cin[c], x1s[core, c]
-            cout[c] = through * x + (other_factor * own + x1r[c])
-            x2s[c] = own_factor * x + own
-
-        @pl.when(passes)
-        def _():
-            chain(h, chain_to).start()
-
-        back(h).start()
-        return carry
-
-    relay_turn = lax.div(far, 5)
-
-    def turn(t, carry):
-        @pl.when(t == relay_turn)
-        def _():
-            lax.fori_loop(0, HARM, relay, 0)
-
-        @pl.when(t == 0)
-        def _():
-            lax.fori_loop(0, HARM, eliminate, 0)
-
-        return carry
-
-    lax.fori_loop(0, 2, turn, 0)
+
+        def one_piece(k, carry):
+            swap(k).wait_recv()
+            owns, offers = [], []
+            for m in range(PIECE):
+                c = k * PIECE + m
+                own = x1s[core, c] + part * x1s[1 - core, c]
+                xt[core, c] = own
+                owns.append(own)
+                offers.append(other_factor * own + x1r[c])
+
+            @pl.when(gets)
+            def _():
+                chain(k, chain_from).wait_recv()
+
+            for m in range(PIECE):
+                c = k * PIECE + m
+                x = cin[c]
+                cout[c] = through * x + offers[m]
+                x2s[c] = own_factor * x + owns[m]
+
+            @pl.when(passes)
+            def _():
+                chain(k, chain_to).start()
+
+            back(k).start()
+            return carry
+
+        lax.fori_loop(0, PIECES, one_piece, 0)
+
+    @pl.when(far >= 4)
+    def _():
+        give()
+        serve_pivots()
+
+    @pl.when(far < chips - 1)
+    def _():
+        relay_all()
+
+    @pl.when(far < 4)
+    def _():
+        give()
+
+    e_in = jnp.where(lower, mi[1], mi[0])
+    f_in = jnp.where(lower, mi[0], mi[1])
+    n, m = e_in, one
+    for i in range(ROWS):
+        n = n + dlt[i] * m
+        after = n + m
+        inv = 1.0 / after
+        qq[i] = m * inv
+        ww[i] = inv
+        m = after
+    e_out = n * inv
+    ends[0] = inv
+    ends[1] = 1.0 - f_in
+    ends[2] = 1.0 / (e_out + f_in * qq[ROWS - 1])
+
+    lax.fori_loop(0, HARM, eliminate, 0)
+
+    @pl.when(far == chips - 1)
+    def _():
+        relay_all()
 
     def finish_copy(h):
         part = pl.ds(h * VARS, VARS)
         return pltpu.make_async_copy(bb.at[:, part], out_hbm.at[:, part], out_sem.at[h])
 
     def finish(h, carry):
-        back(h).wait_recv()
+        def returned(k, carry):
+            back(k).wait_recv()
+            return carry
+
+        first = lax.div(h * VARS + PIECE - 1, PIECE)
+        last = lax.div((h + 1) * VARS + PIECE - 1, PIECE)
+        lax.fori_loop(first, last, returned, 0)
         entering, after = [], []
         for v in range(VARS):
             c = h * VARS + v
             held, given = cin[c], x2r[c]
             p = jnp.where(lower, held, given)
             r = jnp.where(lower, given, held)
-            whole = ends[0] * p + x1s[0, c]
+            whole = ends[0] * p + xt[0, c]
             entering.append(p)
-            after.append((r + ends[2] * whole) * ends[3])
+            after.append((r + ends[1] * whole) * ends[2])
 
         def back_row(t, after):
             i = ROWS - 1 - t
@@ -746,7 +773,6 @@
 
     pitch_next.wait_send()
     pitch_prev.wait_send()
-    send_ends.wait_send()
 
     @pl.when(rad > 0)
     def _():
@@ -767,15 +793,20 @@
         def _():
             radial_down(h, rad - 1).wait_send()
 
+        return carry
+
+    lax.fori_loop(0, HARM, sent_pieces, 0)
+
+    def sent_chain(k, carry):
         @pl.when(passes)
         def _():
-            chain(h, chain_to).wait_send()
-
-        swap(h).wait_send()
-        back(h).wait_send()
-        return carry
-
-    lax.fori_loop(0, HARM, sent_pieces, 0)
+            chain(k, chain_to).wait_send()
+
+        swap(k).wait_send()
+        back(k).wait_send()
+        return carry
+
+    lax.fori_loop(0, PIECES, sent_chain, 0)
 
     def written(h, carry):
         finish_copy(h).wait()
@@ -840,14 +871,15 @@
                 vmem(ROWS),
                 vmem(ROWS + 2),
                 vmem(2, 4),
-                vmem(4),
+                vmem(3),
                 vmem(2),
-                vmem(2, HV),
-                vmem(HV),
-                vmem(HV),
-                vmem(HV),
-                vmem(HV),
-                vmem(HV),
+                vmem(2, PAD),
+                vmem(2, PAD),
+                vmem(PAD),
+                vmem(PAD),
+                vmem(PAD),
+                vmem(PAD),
+                vmem(PAD),
                 vmem(2, ROWS),
                 vmem(2, 2, 4),
                 vmem(2, 2, 4),
@@ -863,14 +895,12 @@
                 dma((2,)),
                 dma((3,)),
                 dma((3,)),
-                dma,
-                dma,
-                dma((HARM,)),
-                dma((HARM,)),
-                dma((HARM,)),
-                dma((HARM,)),
-                dma((HARM,)),
-                dma((HARM,)),
+                dma((PIECES,)),
+                dma((PIECES,)),
+                dma((PIECES,)),
+                dma((PIECES,)),
+                dma((PIECES,)),
+                dma((PIECES,)),
                 dma((2,)),
                 dma((2,)),
                 dma((2,)),

time: 50.7 us -> 45.1 us (0.89)
  Pallas kernels: 48.9 us -> 43.3 us
    pallas_call x1, Pallas kernels: 48.9 us -> 43.3 us  [on_device(): pl.pallas_call(functools.partial(kernel, sizes), out_shape=jax.ShapeDtype...]
where the time goes in v5:
time: 45.1 us; the launch traced here: 45 us
  Pallas kernels  43.3 us (96%)
  local copies, waits for them, and re-layouts  1.69 us (4%)
    pallas_call x1, Pallas kernels, on_device(): pl.pallas_call(functools.partial(kernel, sizes), out_shape=jax.ShapeDtype...  43.3 us
    unnamed x1, local copies, waits for them, and re-layouts  1.69 us

profile of v5, /device:TPU:1, one launch (start us, length us, event | category | flops | bytes accessed | tf_op | source)
XLA Modules:
  0.0 45.0 jit_solution(6838880632748378793)
XLA Ops:
  0.0 43.3 %shard_map.46 = f32[16,49,8,128]{3,2,1,0:T(8,128)S(1)} custom-call(f32[16,49,8,128]{3,2,1,0:T(8,128)} %bitcast.21, f32[3,7,7]{2,1,0:T(8,128)} %jac_hbm.1, f32[8,128]{1,0:T(8,128)} %bitcast.23, s32[16,8,128]{2,1,0:T(8,128)} %bitcast.22), custom_call_target="tpu_custom_call" | custom-call | tf_op jit(solution)/shard_map/pallas_call | solution.py:842
  43.3 1.7 %copy.10 = f32[16,49,4,256]{3,2,1,0:T(4,128)} copy(f32[16,49,4,256]{3,2,1,0:T(4,128)S(1)} %bitcast.20) | data formatting | bytes 6422528

commit v6 on v5

--- a/solution.py
+++ b/solution.py
@@ -42,7 +42,7 @@
     jac_hbm,
     line_hbm,
     mask_hbm,
-    out_hbm,
+    out,
     jac,
     line,
     mask,
@@ -79,7 +79,6 @@
     part_s,
     part_r,
     in_sem,
-    out_sem,
     a_send,
     a_recv,
     r_send,
@@ -717,10 +716,6 @@
     def _():
         relay_all()
 
-    def finish_copy(h):
-        part = pl.ds(h * VARS, VARS)
-        return pltpu.make_async_copy(bb.at[:, part], out_hbm.at[:, part], out_sem.at[h])
-
     def finish(h, carry):
         def returned(k, carry):
             back(k).wait_recv()
@@ -747,11 +742,10 @@
                 c = h * VARS + v
                 x = (bb[i, c] + w * entering[v]) + q * after[v]
                 following.append(x)
-                bb[i, c] = st[1 + i, c] + x
+                out[i, c] = st[1 + i, c] + x
             return tuple(following)
 
         lax.fori_loop(0, ROWS, back_row, tuple(after))
-        finish_copy(h).start()
         return carry
 
     lax.fori_loop(0, HARM, finish, 0)
@@ -807,12 +801,6 @@
         return carry
 
     lax.fori_loop(0, PIECES, sent_chain, 0)
-
-    def written(h, carry):
-        finish_copy(h).wait()
-        return carry
-
-    lax.fori_loop(0, HARM, written, 0)
 
 
 def solution(mesh):
@@ -848,7 +836,7 @@
                 pl.BlockSpec(memory_space=pltpu.HBM),
                 pl.BlockSpec(memory_space=pltpu.HBM),
             ],
-            out_specs=pl.BlockSpec(memory_space=pl.ANY),
+            out_specs=pl.BlockSpec(memory_space=pltpu.VMEM),
             scratch_shapes=[
                 pltpu.SMEM((3, VARS, VARS), F32),
                 vmem(),
@@ -886,7 +874,6 @@
                 vmem(2, HARM, 4),
                 vmem(2, HARM, 4),
                 dma((4,)),
-                dma((HARM,)),
                 dma((2,)),
                 dma((2,)),
                 dma((2, HARM)),

time: 45.1 us -> 44.7 us (level)
  no operation moved by 1% of the time
where the time goes in v6:
time: 44.7 us; the launch traced here: 44.6 us
  Pallas kernels  42.9 us (96%)
  local copies, waits for them, and re-layouts  1.69 us (4%)
    pallas_call x1, Pallas kernels, on_device(): pl.pallas_call(functools.partial(kernel, sizes), out_shape=jax.ShapeDtype...  42.9 us
    unnamed x1, local copies, waits for them, and re-layouts  1.69 us

profile of v6, /device:TPU:1, one launch (start us, length us, event | category | flops | bytes accessed | tf_op | source)
XLA Modules:
  0.0 44.6 jit_solution(12317880776132385434)
XLA Ops:
  0.0 42.9 %shard_map.46 = f32[16,49,8,128]{3,2,1,0:T(8,128)S(1)} custom-call(f32[16,49,8,128]{3,2,1,0:T(8,128)} %bitcast.21, f32[3,7,7]{2,1,0:T(8,128)} %jac_hbm.1, f32[8,128]{1,0:T(8,128)} %bitcast.23, s32[16,8,128]{2,1,0:T(8,128)} %bitcast.22), custom_call_target="tpu_custom_call" | custom-call | tf_op jit(solution)/shard_map/pallas_call | solution.py:830
  42.9 1.7 %copy.10 = f32[16,49,4,256]{3,2,1,0:T(4,128)} copy(f32[16,49,4,256]{3,2,1,0:T(4,128)S(1)} %bitcast.20) | data formatting | bytes 6422528

commit v7 on v6

--- a/solution.py
+++ b/solution.py
@@ -482,7 +482,7 @@
                 bb[i, h * VARS + v] = t
 
     def inner_rows(step, carry):
-        @pl.when(step == 6)
+        @pl.when(step == 10)
         def _():
             return_sums()
 

time: 44.7 us -> 44.5 us (level)
  no operation moved by 1% of the time
where the time goes in v7:
time: 44.5 us; the launch traced here: 44.4 us
  Pallas kernels  42.7 us (96%)
  local copies, waits for them, and re-layouts  1.69 us (4%)
    pallas_call x1, Pallas kernels, on_device(): pl.pallas_call(functools.partial(kernel, sizes), out_shape=jax.ShapeDtype...  42.7 us
    unnamed x1, local copies, waits for them, and re-layouts  1.69 us

profile of v7, /device:TPU:1, one launch (start us, length us, event | category | flops | bytes accessed | tf_op | source)
XLA Modules:
  0.0 44.4 jit_solution(8023333456064371212)
XLA Ops:
  0.0 42.7 %shard_map.46 = f32[16,49,8,128]{3,2,1,0:T(8,128)S(1)} custom-call(f32[16,49,8,128]{3,2,1,0:T(8,128)} %bitcast.21, f32[3,7,7]{2,1,0:T(8,128)} %jac_hbm.1, f32[8,128]{1,0:T(8,128)} %bitcast.23, s32[16,8,128]{2,1,0:T(8,128)} %bitcast.22), custom_call_target="tpu_custom_call" | custom-call | tf_op jit(solution)/shard_map/pallas_call | solution.py:830
  42.8 1.7 %copy.10 = f32[16,49,4,256]{3,2,1,0:T(4,128)} copy(f32[16,49,4,256]{3,2,1,0:T(4,128)S(1)} %bitcast.20) | data formatting | bytes 6422528
